TPU v7x, 32 devices: a whole 2x2x4 slice. The times are simulated.
32 devices in a mesh: ctx: 4 (over y, core), head: 2 (over x), dp: 4 (over z).
Axes of the slice: x: 2, y: 2, z: 4, core: 2. Of those that a mesh axis runs over, the one named last changes fastest.
Arguments:
- queries: bfloat16 [1024, 6144], P(('dp', 'ctx', 'head')), parts along dimension 0, may hold values from -18 to 18
- keys: bfloat16 [1024, 1024], P(('dp', 'ctx', 'head')), parts along dimension 0, may hold values from -9 to 9
- values: bfloat16 [1024, 1024], P(('dp', 'ctx', 'head')), parts along dimension 0, may hold values from -6 to 6
- level_gain: float32 [64, 6144], P(None, 'head'), may hold values from 0.5 to 4
- levels: int32 [16], P('dp'), parts along dimension 0, may hold values from 0 to 63
- visible: int32 [16, 4], P('dp'), parts along dimension 0, may hold values from 0 to 1, as said below
- counts: int32 [16], P('dp'), parts along dimension 0, may hold values from 32 to 64, as said below
Outputs:
- mixed: bfloat16 [1024, 6144], P(('dp', 'ctx', 'head')), parts along dimension 0
- finished: bfloat16 [256, 6144], P(('dp', 'ctx'), 'head'), parts along dimension 0
There are 4 independent parts, one for each index of `dp`. A program takes and returns all parts, laid end to end along the dimension named above; an argument that names none is the same for every part. Nothing has to cross between parts.
Inputs may be any that keep to these rules, and one draw needn't show every extreme that they name: visible[c][c] is 1, visible[c][d] is 0 for d > c, and entries below the diagonal are 0 or 1. `counts`: every clip has at least half of its slots live, and in every draw some clip has all 64 live.
All inputs are finite; a program needn't handle non-finite values.
Results may differ from a plain program's by a relative error of at most 0.0045.
Values may be sent and summed in bfloat16 or wider, within the bound.
No kernel may reach another device: no remote copies, remote signals or barrier semaphores. Data moves between devices by JAX's collectives and lax.ppermute only.
A program may use at most 64 MiB of HBM per device.

v0:
```python
import math

import jax
import jax.numpy as jnp
from jax import lax
from jax.sharding import PartitionSpec as P

QUERY_HEADS = 48
KEY_VALUE_HEADS = 8
HEAD_SIZE = 128
LEVELS = 64
CLIPS = 4


def from_behind(block, axis, distance):
    devices = range(lax.axis_size(axis))
    route = [(i - distance, i) for i in devices if i - distance in devices]
    return lax.ppermute(block, axis, route)


def body(queries, keys, values, level_gain, levels, visible, counts):
    head_count = lax.axis_size("head")
    ctx_count = lax.axis_size("ctx")
    ctx_index = lax.axis_index("ctx")
    tok_rows = queries.shape[0]
    rows_ctx = tok_rows * head_count
    clip_tok = rows_ctx * ctx_count // CLIPS
    heads_per_group = QUERY_HEADS // KEY_VALUE_HEADS
    scale = 1.0 / math.sqrt(HEAD_SIZE)
    clip_range = jnp.arange(CLIPS, dtype=jnp.int32)
    source_count = ctx_count // CLIPS
    query_local, key_local, value_local = (
        lax.all_to_all(queries, "head", split_axis=1, concat_axis=0, tiled=True),
        lax.all_to_all(keys, "head", split_axis=1, concat_axis=0, tiled=True),
        lax.all_to_all(values, "head", split_axis=1, concat_axis=0, tiled=True),
    )
    query_width = query_local.shape[1]
    query_ids = ctx_index * rows_ctx + jnp.arange(rows_ctx, dtype=jnp.int32)
    row_groups = [(0, rows_ctx)]
    query_grouped = query_local.reshape(rows_ctx, -1, heads_per_group, HEAD_SIZE)
    local_kv_heads = query_grouped.shape[1]
    query_onehot = (query_ids // clip_tok)[:, None] == clip_range[None, :]
    query_count = jnp.sum(jnp.where(query_onehot, counts[None, :], 0), axis=1)
    query_live = query_ids % clip_tok < query_count
    query_sees = jnp.sum(jnp.where(query_onehot[:, :, None], visible[None, :, :], 0), axis=1) == 1
    query_level = jnp.sum(jnp.where(query_onehot, levels[None, :], 0), axis=1)

    def key_block(carry_state, key_block_rows, value_block_rows, first_row):
        block_rows = key_block_rows.shape[0]
        key_ids = first_row + jnp.arange(block_rows, dtype=jnp.int32)
        key_onehot = (key_ids // clip_tok)[:, None] == clip_range[None, :]
        key_count = jnp.sum(jnp.where(key_onehot, counts[None, :], 0), axis=1)
        key_live = key_ids % clip_tok < key_count
        block_clips = jnp.any(key_onehot & key_live[:, None], axis=0)
        key_head_rows = key_block_rows.reshape(block_rows, -1, HEAD_SIZE)
        value_head_rows = value_block_rows.reshape(block_rows, -1, HEAD_SIZE)
        group_start, group_rows = row_groups[0]
        group_end = group_start + group_rows
        part_state = tuple((member for member in carry_state))
        group_sees = query_sees
        needed = jnp.any(jnp.any(group_sees, axis=0) & block_clips)

        def update(state, group_sees=group_sees, group_start=group_start, group_end=group_end):
            running_max, denominator, weighted = state
            allowed = (
                jnp.any(group_sees[:, None, :] & key_onehot[None, :, :], axis=-1)
                & key_live[None, :]
            )
            scores = (
                jnp.einsum(
                    "rkgd,nkd->rkgn",
                    query_grouped,
                    key_head_rows,
                    preferred_element_type=jnp.float32,
                )
                * scale
            )
            key_mask = allowed[:, None, None, :]
            scores = jnp.where(key_mask, scores, -1e30)
            new_max = jnp.maximum(running_max, jnp.max(scores, axis=-1))
            weights = jnp.where(key_mask, jnp.exp(scores - new_max[..., None]), 0.0)
            shrink = jnp.exp(running_max - new_max)
            denominator = denominator * shrink + jnp.sum(weights, axis=-1)
            weighted = weighted * shrink[..., None] + jnp.einsum(
                "rkgn,nkd->rkgd",
                weights.astype(jnp.bfloat16),
                value_head_rows,
                preferred_element_type=jnp.float32,
            )
            return (new_max, denominator, weighted)

        def keep(state):
            return state

        group_states = [lax.cond(needed, update, keep, part_state)]
        if len(group_states) == 1:
            return group_states[0]
        return tuple(
            (
                jnp.concatenate([state[member] for state in group_states], axis=0)
                for member in range(3)
            )
        )

    initial = (
        jnp.full((rows_ctx, local_kv_heads, heads_per_group), -1e30, jnp.float32),
        jnp.zeros((rows_ctx, local_kv_heads, heads_per_group), jnp.float32),
        jnp.zeros((rows_ctx, local_kv_heads, heads_per_group, HEAD_SIZE), jnp.float32),
    )
    key_piece = lax.all_gather(key_local, "ctx", axis=0, tiled=True)
    value_piece = lax.all_gather(value_local, "ctx", axis=0, tiled=True)
    piece_rows = key_piece.shape[0]
    block_rows = math.gcd(piece_rows, 512)

    def advance(block_index, inner_state):
        key_slice = lax.dynamic_slice_in_dim(key_piece, block_index * block_rows, block_rows, 0)
        value_slice = lax.dynamic_slice_in_dim(value_piece, block_index * block_rows, block_rows, 0)
        return key_block(inner_state, key_slice, value_slice, block_index * block_rows)

    final_state = lax.fori_loop(0, piece_rows // block_rows, advance, initial)
    attended = (final_state[2] / final_state[1][..., None]).reshape(rows_ctx, query_width)
    level_onehot = (query_level[:, None] == jnp.arange(LEVELS, dtype=jnp.int32)[None, :]).astype(
        jnp.float32
    )
    gate_rows = jnp.dot(
        level_onehot,
        level_gain,
        precision=lax.Precision.HIGHEST,
        preferred_element_type=jnp.float32,
    )
    gated = jnp.where(query_live[:, None], attended * gate_rows, 0.0).astype(jnp.bfloat16)
    mixed = lax.all_to_all(gated, "head", split_axis=0, concat_axis=1, tiled=True)
    relay_rows = rows_ctx // CLIPS
    held = jnp.where(ctx_index < source_count, gated, jnp.zeros_like(gated)).reshape(
        CLIPS, relay_rows, query_width
    )
    empty_block = jnp.zeros_like(held)
    sources = jnp.arange(source_count, dtype=jnp.int32)
    hop_bits = (source_count - 1).bit_length()
    for bit_number in reversed(range(hop_bits)):
        higher = sources >> bit_number + 1 << bit_number + 1
        places = sources + 3 * higher
        holds_bit = jnp.any((places == ctx_index) & (sources >> bit_number & 1 == 1))
        moving = jnp.where(holds_bit, held, empty_block)
        staying = jnp.where(holds_bit, empty_block, held)
        arriving = from_behind(moving, "ctx", 3 * (1 << bit_number))
        held = staying + arriving
    group_position = ctx_index % CLIPS
    finished = held[0]
    for lane_number in range(1, CLIPS):
        arriving_tile = from_behind(held[lane_number], "ctx", lane_number)
        finished = jnp.where(group_position == lane_number, arriving_tile, finished)
    return (mixed, finished)


def solution(mesh):
    placed = (
        P(("dp", "ctx", "head"), None),
        P(("dp", "ctx", "head"), None),
        P(("dp", "ctx", "head"), None),
        P(None, "head"),
        P("dp"),
        P("dp", None),
        P("dp"),
    )
    return jax.shard_map(
        body,
        mesh=mesh,
        in_specs=placed,
        out_specs=(P(("dp", "ctx", "head"), None), P(("dp", "ctx"), "head")),
        check_vma=False,
    )
```

profile of v0, /device:TPU:0, one launch (start us, length us, event | category | flops | bytes accessed | tf_op | source)
XLA Modules:
  0.0 61.5 jit_solution(9454937511669953927)
XLA Ops:
  0.6 0.0 copy-start
  0.6 1.5 %copy.71 = bf16[4,2,8,512]{3,2,0,1:T(8,128)(2,1)} copy(bf16[4,2,8,512]{3,2,1,0:T(8,128)(2,1)} %bitcast.40) | data formatting | bytes 131072 | tf_op jit(solution)/shard_map/all_to_all | solution.py:34
  2.2 4.2 %all-to-all-start = ((bf16[32,2,512]{2,0,1:T(8,128)(2,1)}), bf16[32,2,512]{2,0,1:T(8,128)(2,1)S(1)}, u32[]{:S(2)}, u32[]{:S(2)}) async-start(bf16[32,2,512]{2,0,1:T(8,128)(2,1)} %bitcast.31), calls=%async_computation | async-start | bytes 131072 | tf_op jit(solution)/shard_map/all_to_all | solution.py:34
  6.5 0.8 %select_reduce_fusion = s32[64,4]{0,1:T(4,128)S(1)} fusion(s32[4,4]{1,0:T(4,128)} %param.14, pred[64,4]{0,1:T(4,128)(4,1)S(1)} %iota_compare_fusion.3), kind=kLoop, calls=%fused_computation.33 | loop fusion | flops 1792 | bytes 1344 | tf_op jit(solution)/shard_map/reduce_sum | solution.py:45
  7.2 0.1 fusion.20
  7.3 0.7 %select_reduce_fusion.1 = s32[256]{0:T(256)S(1)} fusion(s32[4]{0:T(128)} %param.15, s32[256]{0:T(256)S(1)} %and_select_fusion.2), kind=kLoop, calls=%fused_computation.34 | loop fusion | flops 2816 | bytes 2064 | tf_op jit(solution)/shard_map/while/body/eval_jaxpr/reduce_sum | solution.py:52
  8.1 0.1 iota_compare_fusion.2
  8.2 0.8 %select_reduce_fusion.2 = (s32[64]{0:T(128)S(1)}, s32[64]{0:T(128)S(1)}) fusion(s32[4]{0:T(128)} %param.13, s32[64]{0:T(128)S(1)} %and_select_fusion.3, s32[4]{0:T(128)} %param.15), kind=kLoop, calls=%fused_computation.37 | loop fusion | flops 1152 | bytes 800 | tf_op jit(solution)/shard_map/reduce_sum | solution.py:46
  9.0 0.6 %and_reduce_fusion.2 = pred[]{:T(512)} fusion(pred[4]{0:T(512)(128)(4,1)S(1)} %get-tuple-element.148, pred[4]{0:T(512)(128)(4,1)S(1)} %get-tuple-element.158), kind=kLoop, calls=%fused_computation.43 | loop fusion | flops 7 | bytes 9 | tf_op jit(solution)/shard_map/while/body/eval_jaxpr/reduce_or | solution.py:61
  9.6 1.5 %copy.70 = bf16[4,2,8,512]{3,2,0,1:T(8,128)(2,1)} copy(bf16[4,2,8,512]{3,2,1,0:T(8,128)(2,1)} %bitcast.41) | data formatting | bytes 131072 | tf_op jit(solution)/shard_map/all_to_all | solution.py:35
  11.1 0.0 all-to-all-done
  11.1 3.3 %all-to-all-start.2 = ((bf16[32,2,512]{2,0,1:T(8,128)(2,1)}), bf16[32,2,512]{2,0,1:T(8,128)(2,1)S(1)}, u32[]{:S(2)}, u32[]{:S(2)}) async-start(bf16[32,2,512]{2,0,1:T(8,128)(2,1)} %bitcast.30), calls=%async_computation.2 | async-start | bytes 131072 | tf_op jit(solution)/shard_map/all_to_all | solution.py:35
  15.1 1.8 %copy.69 = bf16[4,2,8,3072]{3,2,0,1:T(8,128)(2,1)} copy(bf16[4,2,8,3072]{3,2,1,0:T(8,128)(2,1)} %bitcast.35) | data formatting | bytes 786432 | tf_op jit(solution)/shard_map/all_to_all | solution.py:33
  16.8 0.1 broadcast_in_dim.139
  16.9 1.6 %all-to-all-done.2 = bf16[32,2,512]{2,0,1:T(8,128)(2,1)S(1)} async-done(((bf16[32,2,512]{2,0,1:T(8,128)(2,1)}), bf16[32,2,512]{2,0,1:T(8,128)(2,1)S(1)}, u32[]{:S(2)}, u32[]{:S(2)}) %all-to-all-start.2) | async-done | bytes 65568 | tf_op jit(solution)/shard_map/all_to_all | solution.py:35
  18.5 3.5 %all-to-all-start.1 = ((bf16[32,2,3072]{2,0,1:T(8,128)(2,1)}), bf16[32,2,3072]{2,0,1:T(8,128)(2,1)S(1)}, u32[]{:S(2)}, u32[]{:S(2)}) async-start(bf16[32,2,3072]{2,0,1:T(8,128)(2,1)} %bitcast.29), calls=%async_computation.1 | async-start | bytes 786432 | tf_op jit(solution)/shard_map/all_to_all | solution.py:33
  22.0 6.3 %all_gather.6 = bf16[256,512]{1,0:T(8,128)(2,1)S(1)} all-gather(bf16[64,512]{1,0:T(8,128)(2,1)S(1)} %bitcast.37), channel_id=1, replica_groups=mesh['ctx'=4,'head'=2,'dp'=4] {'ctx'}, dimensions={0}, use_global_device_ids=true | all-gather | bytes 327680 | tf_op jit(solution)/shard_map/all_gather | solution.py:110
  28.3 5.8 %all_gather.7 = bf16[256,512]{1,0:T(8,128)(2,1)S(1)} all-gather(bf16[64,512]{1,0:T(8,128)(2,1)S(1)} %bitcast.38), channel_id=1, replica_groups=mesh['ctx'=4,'head'=2,'dp'=4] {'ctx'}, dimensions={0}, use_global_device_ids=true | all-gather | bytes 327680 | tf_op jit(solution)/shard_map/all_gather | solution.py:111
  34.2 0.0 all-to-all-done.1
  34.2 6.7 %conditional.1 = ((f32[64,4,6]{0,2,1:T(8,128)S(1)}, f32[64,4,6,128]{3,0,2,1:T(8,128)S(1)})) conditional(s32[]{:T(128)} %convert_element_type.13, (f32[64,4,6]{0,2,1:T(8,128)S(1)}, f32[64,4,6,128]{3,0,2,1:T(8,128)S(1)}) %tuple.31, (pred[64,4]{0,1:T(4,128)(4,1)S(1)}, pred[256,4]{0,1:T(4,128)(4,1)S(1)}, s32[256]{0:T(256)S(1)}, s32[256]{0:T(256)S(1)}, ...), branch_computations={%region_6.7_spmd, %region_7.11_spmd} | conditional | flops 205395968 | bytes 9220888 | solution.py:95
  34.2 1.3 %reshape.148 = bf16[64,4,6,128]{3,2,1,0:T(8,128)(2,1)} reshape(bf16[2,32,3072]{2,1,0:T(8,128)(2,1)S(1)} %get-tuple-element.127) | data formatting | bytes 786432 | tf_op jit(solution)/shard_map/reshape | solution.py:40
  35.4 0.8 %reshape.147 = bf16[256,4,128]{2,1,0:T(4,128)(2,1)} reshape(bf16[256,512]{1,0:T(8,128)(2,1)S(1)} %get-tuple-element.126) | data formatting | bytes 524288 | tf_op jit(solution)/shard_map/while/body/eval_jaxpr/reshape | solution.py:55
  36.2 0.1 and_reduce_fusion
  36.4 1.6 %fusion.21 = (f32[64,4,6]{0,2,1:T(8,128)S(1)}, f32[64,4,6,256]{3,0,2,1:T(8,128)S(1)}) fusion(bf16[64,4,6,128]{3,2,1,0:T(8,128)(2,1)} %reshape.148, bf16[256,4,128,1]{2,1,0,3:T(4,128)(2,1)} %bitcast.39, pred[64,256]{1,0:T(8,128)(4,1)S(1)} %broadcast_and_fusion), kind=kOutput, calls=%fused_computation.57 | convolution fusion | flops 101841408 | bytes 2250752 | tf_op jit(solution)/shard_map/while/body/eval_jaxpr/cond/branch_1_fun/rkgd,nkd->rkgn/dot_general | solution.py:70
  38.0 0.5 fusion.2
  38.6 0.8 %reshape.149 = bf16[256,4,128]{2,1,0:T(4,128)(2,1)} reshape(bf16[256,512]{1,0:T(8,128)(2,1)S(1)} %get-tuple-element.129) | data formatting | bytes 524288 | tf_op jit(solution)/shard_map/while/body/eval_jaxpr/reshape | solution.py:56
  39.3 1.6 %fusion = f32[64,4,6,128]{3,0,2,1:T(8,128)S(1)} fusion(f32[64,4,6,256]{3,0,2,1:T(8,128)S(1)} %get-tuple-element.153, f32[64,4,6,128]{3,0,2,1:T(8,128)S(1)} %get-tuple-element.128, f32[64,4,6]{0,2,1:T(8,128)S(1)} %broadcast_maximum_fusion, pred[64,256]{1,0:T(8,128)(4,1)S(1)} %broadcast_and_fusion, f32[64,4,6]{0,2,1:T(8,128)S(1)} %get-tuple-element.150, ...), kind=kOutput, calls=%fused_computation.3 | convolution fusion | flops 102236160 | bytes 3436544 | tf_op jit(solution)/shard_map/while/body/eval_jaxpr/cond/branch_1_fun/rkgn,nkd->rkgd/dot_general | solution.py:84
  40.9 0.3 broadcast_divide_fusion
  41.2 0.5 copy.44
  41.7 0.2 reshape.151
  41.9 0.0 copy-done
  41.9 1.3 %broadcast_select_fusion = (bf16[64,3072]{1,0:T(8,128)(2,1)S(1)}, bf16[64,3072]{1,0:T(8,128)(2,1)}) fusion(pred[]{:T(512)S(6)} %lt.53, f32[64,3072]{1,0:T(8,128)S(1)} %reshape.151, f32[64,3072]{1,0:T(8,128)S(1)} %copy-done, s32[64]{0:T(128)S(1)} %get-tuple-element.146, pred[64]{0:T(512)(128)(4,1)S(1)} %fusion.19), kind=kOutput, calls=%fused_computation.25 | convolution fusion | flops 151785472 | bytes 2359617 | tf_op jit(solution)/shard_map/dot_general | solution.py:125
  43.2 3.4 %collective-permute-start = (bf16[16,3072]{1,0:T(8,128)(2,1)S(1)}, bf16[16,3072]{1,0:T(8,128)(2,1)S(1)}, u32[]{:S(2)}, u32[]{:S(2)}) collective-permute-start(bf16[16,3072]{1,0:T(8,128)(2,1)S(1)} %get-tuple-element.156), channel_id=1, source_target_pairs={{0,24},{1,25},{2,26},{3,27},{4,28},{5,29},{6,30},{7,31}} | collective-permute-start | bytes 294920 | tf_op jit(solution)/shard_map/ppermute | solution.py:18
  46.6 1.3 %collective-permute-start.1 = (bf16[16,3072]{1,0:T(8,128)(2,1)S(1)}, bf16[16,3072]{1,0:T(8,128)(2,1)S(1)}, u32[]{:S(2)}, u32[]{:S(2)}) collective-permute-start(bf16[16,3072]{1,0:T(8,128)(2,1)S(1)} %get-tuple-element.155), channel_id=1, source_target_pairs={{0,16},{8,24},{1,17},{9,25},{2,18},{10,26},{3,19},{11,27},{4,20},{... | collective-permute-start | bytes 294920 | tf_op jit(solution)/shard_map/ppermute | solution.py:18
  47.9 2.0 %collective-permute-start.2 = (bf16[16,3072]{1,0:T(8,128)(2,1)S(1)}, bf16[16,3072]{1,0:T(8,128)(2,1)S(1)}, u32[]{:S(2)}, u32[]{:S(2)}) collective-permute-start(bf16[16,3072]{1,0:T(8,128)(2,1)S(1)} %get-tuple-element.154), channel_id=1, source_target_pairs={{0,8},{8,16},{16,24},{1,9},{9,17},{17,25},{2,10},{10,18},{18,26},{... | collective-permute-start | bytes 294920 | tf_op jit(solution)/shard_map/ppermute | solution.py:18
  50.0 3.5 %all-to-all-start.3 = ((bf16[2,32,3072]{2,1,0:T(8,128)(2,1)}), bf16[2,32,3072]{2,1,0:T(8,128)(2,1)S(1)}, u32[]{:S(2)}, u32[]{:S(2)}) async-start(bf16[2,32,3072]{2,1,0:T(8,128)(2,1)} %bitcast.9), calls=%async_computation.3 | async-start | bytes 786432 | tf_op jit(solution)/shard_map/all_to_all | solution.py:132
  53.4 0.0 collective-permute-done
  53.4 0.0 collective-permute-done.1
  53.5 0.0 collective-permute-done.2
  53.5 0.7 %fusion.15 = bf16[16,3072]{1,0:T(8,128)(2,1)} fusion(bf16[16,3072]{1,0:T(8,128)(2,1)S(1)} %collective-permute-done, bf16[16,3072]{1,0:T(8,128)(2,1)S(1)} %collective-permute-done.1, bf16[16,3072]{1,0:T(8,128)(2,1)S(1)} %collective-permute-done.2, bf16[64,3072]{1,0:T(8,128)(2,1)S(1)} %get-tuple-element.159, pred[]{:T(512)S(6)} %eq.97, pred[]{:T(512)S(6)} %eq.96, ...), kind=kLoop, calls=%fused_computation.28 | loop fusion | flops 147456 | bytes 491523 | tf_op jit(solution)/shard_map/jit(_where)/select_n | solution.py:152
  54.1 6.6 %all-to-all-done.3 = bf16[2,32,3072]{2,1,0:T(8,128)(2,1)S(1)} async-done(((bf16[2,32,3072]{2,1,0:T(8,128)(2,1)}), bf16[2,32,3072]{2,1,0:T(8,128)(2,1)S(1)}, u32[]{:S(2)}, u32[]{:S(2)}) %all-to-all-start.3) | async-done | bytes 393248 | tf_op jit(solution)/shard_map/all_to_all | solution.py:132
  60.7 0.8 %copy.55 = bf16[2,4,8,3072]{3,2,0,1:T(8,128)(2,1)} copy(bf16[2,4,8,3072]{3,2,1,0:T(8,128)(2,1)S(1)} %bitcast.33) | data formatting | bytes 786432 | tf_op jit(solution)/shard_map/all_to_all | solution.py:132
  (13 shorter events, 0.1 us)
Async XLA Ops:
  0.6 41.2 %copy-start = (f32[64,3072]{1,0:T(8,128)S(1)}, f32[64,3072]{1,0:T(8,128)}, u32[]{:S(2)}) copy-start(f32[64,3072]{1,0:T(8,128)} %param.12) | copy-start | bytes 2359300
  2.2 8.9 %all-to-all-start = ((bf16[32,2,512]{2,0,1:T(8,128)(2,1)}), bf16[32,2,512]{2,0,1:T(8,128)(2,1)S(1)}, u32[]{:S(2)}, u32[]{:S(2)}) async-start(bf16[32,2,512]{2,0,1:T(8,128)(2,1)} %bitcast.31), calls=%async_computation | async-start | bytes 131072 | tf_op jit(solution)/shard_map/all_to_all | solution.py:34
  11.1 7.4 %all-to-all-start.2 = ((bf16[32,2,512]{2,0,1:T(8,128)(2,1)}), bf16[32,2,512]{2,0,1:T(8,128)(2,1)S(1)}, u32[]{:S(2)}, u32[]{:S(2)}) async-start(bf16[32,2,512]{2,0,1:T(8,128)(2,1)} %bitcast.30), calls=%async_computation.2 | async-start | bytes 131072 | tf_op jit(solution)/shard_map/all_to_all | solution.py:35
  18.5 15.6 %all-to-all-start.1 = ((bf16[32,2,3072]{2,0,1:T(8,128)(2,1)}), bf16[32,2,3072]{2,0,1:T(8,128)(2,1)S(1)}, u32[]{:S(2)}, u32[]{:S(2)}) async-start(bf16[32,2,3072]{2,0,1:T(8,128)(2,1)} %bitcast.29), calls=%async_computation.1 | async-start | bytes 786432 | tf_op jit(solution)/shard_map/all_to_all | solution.py:33
  43.2 10.2 %collective-permute-start = (bf16[16,3072]{1,0:T(8,128)(2,1)S(1)}, bf16[16,3072]{1,0:T(8,128)(2,1)S(1)}, u32[]{:S(2)}, u32[]{:S(2)}) collective-permute-start(bf16[16,3072]{1,0:T(8,128)(2,1)S(1)} %get-tuple-element.156), channel_id=1, source_target_pairs={{0,24},{1,25},{2,26},{3,27},{4,28},{5,29},{6,30},{7,31}} | collective-permute-start | bytes 294920 | tf_op jit(solution)/shard_map/ppermute | solution.py:18
  46.6 6.8 %collective-permute-start.1 = (bf16[16,3072]{1,0:T(8,128)(2,1)S(1)}, bf16[16,3072]{1,0:T(8,128)(2,1)S(1)}, u32[]{:S(2)}, u32[]{:S(2)}) collective-permute-start(bf16[16,3072]{1,0:T(8,128)(2,1)S(1)} %get-tuple-element.155), channel_id=1, source_target_pairs={{0,16},{8,24},{1,17},{9,25},{2,18},{10,26},{3,19},{11,27},{4,20},{... | collective-permute-start | bytes 294920 | tf_op jit(solution)/shard_map/ppermute | solution.py:18
  47.9 5.6 %collective-permute-start.2 = (bf16[16,3072]{1,0:T(8,128)(2,1)S(1)}, bf16[16,3072]{1,0:T(8,128)(2,1)S(1)}, u32[]{:S(2)}, u32[]{:S(2)}) collective-permute-start(bf16[16,3072]{1,0:T(8,128)(2,1)S(1)} %get-tuple-element.154), channel_id=1, source_target_pairs={{0,8},{8,16},{16,24},{1,9},{9,17},{17,25},{2,10},{10,18},{18,26},{... | collective-permute-start | bytes 294920 | tf_op jit(solution)/shard_map/ppermute | solution.py:18
  50.0 10.7 %all-to-all-start.3 = ((bf16[2,32,3072]{2,1,0:T(8,128)(2,1)}), bf16[2,32,3072]{2,1,0:T(8,128)(2,1)S(1)}, u32[]{:S(2)}, u32[]{:S(2)}) async-start(bf16[2,32,3072]{2,1,0:T(8,128)(2,1)} %bitcast.9), calls=%async_computation.3 | async-start | bytes 786432 | tf_op jit(solution)/shard_map/all_to_all | solution.py:132
where the time goes:
time: 62.2 us; the launch traced here: 61.5 us
  starting transfers between devices  21.2 us (34%)
  blocking collectives  12.1 us (19%)
  local copies, waits for them, and re-layouts  9.12 us (15%)
  waiting for transfers between devices  8.19 us (13%)
  other arithmetic  4.82 us (8%)
  matrix products  4.5 us (7%)
  between operations  1.43 us (2%)
    ppermute x3, starting transfers between devices, from_behind(): return lax.ppermute(block, axis, route)  6.7 us
    all_to_all x1, waiting for transfers between devices, body(): lax.all_to_all(gated, 'head', split_axis=0, concat_axis=1, tiled=True)  6.56 us
    all_gather x1, blocking collectives, body(): key_piece = lax.all_gather(key_local, 'ctx', axis=0, tiled=True)  6.31 us
    all_gather x1, blocking collectives, body(): value_piece = lax.all_gather(value_local, 'ctx', axis=0, tiled=True)  5.84 us
    all_to_all x1, starting transfers between devices, body(): lax.all_to_all(keys, 'head', split_axis=1, concat_axis=0, tiled=True)  4.23 us
    all_to_all x1, starting transfers between devices, body(): lax.all_to_all(gated, 'head', split_axis=0, concat_axis=1, tiled=True)  3.48 us
    all_to_all x1, starting transfers between devices, body(): lax.all_to_all(queries, 'head', split_axis=1, concat_axis=0, tiled=True)  3.47 us
    all_to_all x1, starting transfers between devices, body(): lax.all_to_all(values, 'head', split_axis=1, concat_axis=0, tiled=True)  3.32 us
  transfers between devices with their start and end apart: 7, of which 2 were waited for; matrix products, arithmetic and copies ran while one was open for 12% of the time, Pallas kernels for 0%

commit v1 on v0

--- a/solution.py
+++ b/solution.py
@@ -1,8 +1,11 @@
+import functools
 import math
 
 import jax
 import jax.numpy as jnp
 from jax import lax
+from jax.experimental import pallas as pl
+from jax.experimental.pallas import tpu as pltpu
 from jax.sharding import PartitionSpec as P
 
 QUERY_HEADS = 48
@@ -18,7 +21,7 @@
     return lax.ppermute(block, axis, route)
 
 
-def body(queries, keys, values, level_gain, levels, visible, counts):
+def general_body(queries, keys, values, level_gain, levels, visible, counts):
     head_count = lax.axis_size("head")
     ctx_count = lax.axis_size("ctx")
     ctx_index = lax.axis_index("ctx")
@@ -153,6 +156,142 @@
     return (mixed, finished)
 
 
+def attention_kernel(
+    counts_ref,
+    visible_ref,
+    query_ref,
+    first_refs,
+    key_refs,
+    value_refs,
+    gain_ref,
+    far_gain_ref,
+    first_gain_ref,
+    mixed_ref,
+    finished_ref,
+):
+    ctx, head = lax.axis_index("ctx"), lax.axis_index("head")
+    rows, width = query_ref.shape
+    half = width // 2
+    first_rows = finished_ref.shape[0]
+    group = QUERY_HEADS // KEY_VALUE_HEADS
+    group_width = group * HEAD_SIZE
+    pieces = len(key_refs)
+    key_count = pieces * rows
+    scale = 1.0 / math.sqrt(HEAD_SIZE)
+
+    lane = lax.broadcasted_iota(jnp.int32, (1, key_count), 1)
+    piece = lane // rows
+    place = jnp.where(piece % 2 == head, 0, rows) + lane % rows
+    bias = jnp.full((1, key_count), -1e30, jnp.float32)
+    first_bias = bias
+    for flip in range(pieces // 2):
+        clip = ctx ^ ((flip % 2) * 2) ^ (flip // 2)
+        here = (piece // 2 == flip) & (place < counts_ref[clip])
+        seen = jnp.where(visible_ref[ctx, clip] == 1, 0.0, -1e30)
+        bias = jnp.where(here, seen, bias)
+        first_bias = jnp.where(here, jnp.where(clip == 0, 0.0, -1e30), first_bias)
+
+    def attend(query_pieces, keys, values, key_bias):
+        stacked = jnp.concatenate(query_pieces, axis=0)
+        scores = lax.dot_general(
+            stacked, keys, (((1,), (1,)), ((), ())), preferred_element_type=jnp.float32
+        )
+        scores = scores * scale + key_bias
+        peak = jnp.max(scores, axis=1, keepdims=True)
+        probs = jnp.exp(scores - peak)
+        denominator = jnp.sum(probs, axis=1, keepdims=True)
+        weighted = jnp.dot(
+            probs.astype(jnp.bfloat16), values, preferred_element_type=jnp.float32
+        )
+        return weighted / denominator
+
+    row = lax.broadcasted_iota(jnp.int32, (rows, 1), 0)
+    live = row + head * rows < counts_ref[ctx]
+    for kv_head in range(KEY_VALUE_HEADS):
+        columns = slice(kv_head * HEAD_SIZE, (kv_head + 1) * HEAD_SIZE)
+        keys = jnp.concatenate([ref[:, columns] for ref in key_refs], axis=0)
+        values = jnp.concatenate([ref[:, columns] for ref in value_refs], axis=0)
+        start = kv_head * group_width
+        spans = [slice(start + g * HEAD_SIZE, start + (g + 1) * HEAD_SIZE) for g in range(group)]
+        attended = attend([query_ref[:, span] for span in spans], keys, values, bias)
+        for g, span in enumerate(spans):
+            side = span.start // half
+            local = slice(span.start - side * half, span.stop - side * half)
+            gain = jnp.where(head == side, gain_ref[:, local], far_gain_ref[:, local])
+            block = attended[g * rows : (g + 1) * rows] * gain
+            mixed_ref[:, span] = jnp.where(live, block, 0.0).astype(mixed_ref.dtype)
+
+    first_row = lax.broadcasted_iota(jnp.int32, (first_rows, 1), 0)
+    first_live = first_row + ctx * first_rows < counts_ref[0]
+    lower, upper = first_rows * (ctx % 2), half * head
+    for kv_head in range(KEY_VALUE_HEADS // 2):
+        start = pl.multiple_of((head * (KEY_VALUE_HEADS // 2) + kv_head) * HEAD_SIZE, HEAD_SIZE)
+        columns = pl.ds(start, HEAD_SIZE)
+        keys = jnp.concatenate([ref[:, columns] for ref in key_refs], axis=0)
+        values = jnp.concatenate([ref[:, columns] for ref in value_refs], axis=0)
+        start = kv_head * group_width
+        spans = [slice(start + g * HEAD_SIZE, start + (g + 1) * HEAD_SIZE) for g in range(group)]
+        query_pieces = []
+        for span in spans:
+            near, near_other, far, far_other = [ref[:, span] for ref in first_refs]
+            own = query_ref[:first_rows, span]
+            even = jnp.where(head == 1, near, jnp.where(ctx == 0, own, far))
+            odd = jnp.where(head == 1, near_other, far_other)
+            query_pieces.append(jnp.where(ctx % 2 == 0, even, odd))
+        attended = attend(query_pieces, keys, values, first_bias)
+        for g, span in enumerate(spans):
+            block = attended[g * first_rows : (g + 1) * first_rows] * first_gain_ref[:, span]
+            finished_ref[:, span] = jnp.where(first_live, block, 0.0).astype(finished_ref.dtype)
+
+
+def paired_body(queries, keys, values, level_gain, levels, visible, counts):
+    axes = ("ctx", "head")
+    places = [(c, h) for c in range(CLIPS) for h in range(2)]
+    ctx = lax.axis_index("ctx")
+    rows, width = queries.shape
+    half = width // 2
+    first_rows = rows * 2 // CLIPS
+
+    def move(block, route):
+        pairs = [(a * 2 + b, c * 2 + d) for (a, b), (c, d) in route]
+        return lax.ppermute(block, axes, pairs)
+
+    beside = [((c, h), (c, 1 - h)) for c, h in places]
+    across = [((c, h), (c ^ 2, h)) for c, h in places]
+    relay = [((c, h), (c, 1 - h)) for c, h in places if c >= 2]
+    partner = [((c, h), (c ^ 1, h)) for c, h in places]
+    across_keys, across_values = move(keys, across), move(values, across)
+    beside_keys, beside_values = move(keys, beside), move(values, beside)
+    relay_keys, relay_values = move(across_keys, relay), move(across_values, relay)
+    near_keys = [keys, beside_keys, across_keys, relay_keys]
+    near_values = [values, beside_values, across_values, relay_values]
+    all_keys = near_keys + [move(block, partner) for block in near_keys]
+    all_values = near_values + [move(block, partner) for block in near_values]
+
+    upper, lower = queries[:first_rows], queries[first_rows:]
+    first_queries = [
+        move(upper[:, half:], [((0, 0), (0, 1)), ((0, 1), (2, 1))]),
+        move(lower[:, half:], [((0, 0), (1, 1)), ((0, 1), (3, 1))]),
+        move(upper[:, :half], [((0, 1), (2, 0))]),
+        move(lower[:, :half], [((0, 0), (1, 0)), ((0, 1), (3, 0))]),
+    ]
+    gain = lax.dynamic_slice_in_dim(level_gain, levels[ctx], 1, 0)
+    first_gain = lax.dynamic_slice_in_dim(level_gain, levels[0], 1, 0)
+    far_gain = move(gain, beside)
+    smem, vmem = pl.BlockSpec(memory_space=pltpu.SMEM), pl.BlockSpec(memory_space=pltpu.VMEM)
+    pieces = len(all_keys)
+    return pl.pallas_call(
+        attention_kernel,
+        out_shape=(
+            jax.ShapeDtypeStruct((rows, width), queries.dtype),
+            jax.ShapeDtypeStruct((first_rows, half), queries.dtype),
+        ),
+        in_specs=[smem, smem, vmem, [vmem] * 4, [vmem] * pieces, [vmem] * pieces, vmem, vmem, vmem],
+        out_specs=(vmem, vmem),
+        name="attention",
+    )(counts, visible, queries, first_queries, all_keys, all_values, gain, far_gain, first_gain)
+
+
 def solution(mesh):
     placed = (
         P(("dp", "ctx", "head"), None),
@@ -163,8 +302,10 @@
         P("dp", None),
         P("dp"),
     )
+    axes = mesh.shape
+    small = axes["ctx"] == CLIPS and axes["head"] == 2
     return jax.shard_map(
-        body,
+        paired_body if small else general_body,
         mesh=mesh,
         in_specs=placed,
         out_specs=(P(("dp", "ctx", "head"), None), P(("dp", "ctx"), "head")),

time: 62.2 us -> 34.9 us (0.56)
  the two profiles are of different devices: /device:TPU:0 before, /device:TPU:21 now
where the time goes in v1:
time: 34.9 us; the launch traced here: 34.5 us
  starting transfers between devices  16.9 us (48%)
  between operations  4.91 us (14%)
  waiting for transfers between devices  4.56 us (13%)
  local copies, waits for them, and re-layouts  4.49 us (13%)
  Pallas kernels  3.59 us (10%)
    ppermute x19, starting transfers between devices, move(): return lax.ppermute(block, axes, pairs)  16.9 us
    ppermute x19, waiting for transfers between devices, move(): return lax.ppermute(block, axes, pairs)  4.56 us
    pallas_call x1, Pallas kernels, paired_body(): pl.pallas_call(attention_kernel, out_shape=(jax.ShapeDtypeStruct((rows, w...  3.59 us
    dynamic_slice x1, local copies, waits for them, and re-layouts, paired_body(): first_gain = lax.dynamic_slice_in_dim(level_gain, levels[0], 1, 0)  1.56 us
    slice x1, local copies, waits for them, and re-layouts, paired_body(): first_gain = lax.dynamic_slice_in_dim(level_gain, levels[0], 1, 0)  1.32 us
    slice x1, local copies, waits for them, and re-layouts, paired_body(): lower[:, :half]  1.06 us
  transfers between devices with their start and end apart: 19, of which 3 were waited for; matrix products, arithmetic and copies ran while one was open for 3% of the time, Pallas kernels for 0%

profile of v1, /device:TPU:21, one launch (start us, length us, event | category | flops | bytes accessed | tf_op | source)
XLA Modules:
  0.0 34.5 jit_solution(15255427546928319002)
XLA Ops:
  0.6 0.0 copy-start.4
  0.6 1.3 %fusion.1 = (s32[1]{0:T(128)}, s32[1]{0:T(128)}) fusion(s32[4]{0:T(128)} %param.11, s32[]{:T(128)S(6)} %select_n.9), kind=kLoop, calls=%fused_computation.3 | loop fusion | bytes 20 | tf_op jit(solution)/shard_map/slice | solution.py:279
  5.8 1.6 %constant_dynamic-slice_fusion = (f32[1,3072]{1,0:T(1,128)}, f32[1,3072]{1,0:T(1,128)S(1)}) fusion(f32[64,3072]{1,0:T(8,128)} %param.10, s32[]{:T(128)S(6)} %select_n.11, s32[]{:T(128)S(6)} %select_n.10), kind=kLoop, calls=%fused_computation | loop fusion | bytes 49160 | tf_op jit(solution)/shard_map/dynamic_slice | solution.py:279
  7.4 1.2 %collective-permute-start.18 = (f32[1,3072]{1,0:T(1,128)S(1)}, f32[1,3072]{1,0:T(1,128)S(1)}, u32[]{:S(2)}, u32[]{:S(2)}) collective-permute-start(f32[1,3072]{1,0:T(1,128)S(1)} %get-tuple-element.3.gain_ref), channel_id=1, source_target_pairs={{0,4},{4,0},{8,12},{12,8},{16,20},{20,16},{24,28},{28,24},{1,5},{5... | collective-permute-start | bytes 36872 | tf_op jit(solution)/shard_map/ppermute | solution.py:257
  8.6 0.0 copy-done.4
  8.6 0.2 collective-permute-start.5
  8.9 0.3 collective-permute-start.4
  9.1 1.5 %collective-permute-start.7 = (bf16[32,1024]{1,0:T(8,128)(2,1)S(1)}, bf16[32,1024]{1,0:T(8,128)(2,1)S(1)}, u32[]{:S(2)}, u32[]{:S(2)}) collective-permute-start(bf16[32,1024]{1,0:T(8,128)(2,1)S(1)} %copy-done.4), channel_id=1, source_target_pairs={{0,8},{4,12},{8,0},{12,4},{16,24},{20,28},{24,16},{28,20},{1,9},{5... | collective-permute-start | bytes 196616 | tf_op jit(solution)/shard_map/ppermute | solution.py:257
  10.7 1.2 %collective-permute-start.12 = (bf16[32,1024]{1,0:T(8,128)(2,1)}, bf16[32,1024]{1,0:T(8,128)(2,1)S(1)}, u32[]{:S(2)}, u32[]{:S(2)}) collective-permute-start(bf16[32,1024]{1,0:T(8,128)(2,1)} %value_refs_0_.1), channel_id=1, source_target_pairs={{0,16},{4,20},{8,24},{12,28},{16,0},{20,4},{24,8},{28,12},{1,17},{... | collective-permute-start | bytes 196616 | tf_op jit(solution)/shard_map/ppermute | solution.py:257
  11.9 0.0 collective-permute-done.18.far_gain_ref
  11.9 1.2 %collective-permute-start.11 = (bf16[32,1024]{1,0:T(8,128)(2,1)}, bf16[32,1024]{1,0:T(8,128)(2,1)S(1)}, u32[]{:S(2)}, u32[]{:S(2)}) collective-permute-start(bf16[32,1024]{1,0:T(8,128)(2,1)} %value_refs_0_.1), channel_id=1, source_target_pairs={{0,4},{4,0},{8,12},{12,8},{16,20},{20,16},{24,28},{28,24},{1,5},{5... | collective-permute-start | bytes 196616 | tf_op jit(solution)/shard_map/ppermute | solution.py:257
  13.1 1.1 %fusion = (bf16[16,3072]{1,0:T(8,128)(2,1)S(1)}, bf16[16,3072]{1,0:T(8,128)(2,1)S(1)}, bf16[16,3072]{1,0:T(8,128)(2,1)S(1)}, bf16[16,3072]{1,0:T(8,128)(2,1)S(1)}) fusion(bf16[32,6144]{1,0:T(8,128)(2,1)} %query_ref.1), kind=kLoop, calls=%fused_computation.2 | loop fusion | bytes 786432 | tf_op jit(solution)/shard_map/slice | solution.py:276
  14.1 0.0 copy-done.20
  14.2 0.0 copy-done.21
  14.2 0.0 collective-permute-done.5.key_refs_2_
  14.2 0.0 copy-start.6
  14.2 1.3 %collective-permute-start.3 = (bf16[16,3072]{1,0:T(8,128)(2,1)S(1)}, bf16[16,3072]{1,0:T(8,128)(2,1)S(1)}, u32[]{:S(2)}, u32[]{:S(2)}) collective-permute-start(bf16[16,3072]{1,0:T(8,128)(2,1)S(1)} %get-tuple-element.4), channel_id=1, source_target_pairs={{0,8},{4,24},{1,9},{5,25},{2,10},{6,26},{3,11},{7,27}} | collective-permute-start | bytes 294920 | tf_op jit(solution)/shard_map/ppermute | solution.py:257
  15.5 0.0 collective-permute-done.4.key_refs_1_
  15.5 0.0 copy-start.7
  15.5 0.7 %collective-permute-start.2 = (bf16[16,3072]{1,0:T(8,128)(2,1)S(1)}, bf16[16,3072]{1,0:T(8,128)(2,1)S(1)}, u32[]{:S(2)}, u32[]{:S(2)}) collective-permute-start(bf16[16,3072]{1,0:T(8,128)(2,1)S(1)} %get-tuple-element.5), channel_id=1, source_target_pairs={{4,16},{5,17},{6,18},{7,19}} | collective-permute-start | bytes 294920 | tf_op jit(solution)/shard_map/ppermute | solution.py:257
  16.2 0.0 collective-permute-done.7.key_refs_4_
  16.2 0.0 copy-done.5
  16.2 0.0 copy-start.8
  16.2 0.6 %collective-permute-start.14 = (bf16[32,1024]{1,0:T(8,128)(2,1)S(1)}, bf16[32,1024]{1,0:T(8,128)(2,1)S(1)}, u32[]{:S(2)}, u32[]{:S(2)}) collective-permute-start(bf16[32,1024]{1,0:T(8,128)(2,1)S(1)} %copy-done.5), channel_id=1, source_target_pairs={{0,8},{4,12},{8,0},{12,4},{16,24},{20,28},{24,16},{28,20},{1,9},{5... | collective-permute-start | bytes 196616 | tf_op jit(solution)/shard_map/ppermute | solution.py:257
  16.8 0.0 collective-permute-done.12.value_refs_2_
  16.8 0.7 %collective-permute-start.1 = (bf16[16,3072]{1,0:T(8,128)(2,1)S(1)}, bf16[16,3072]{1,0:T(8,128)(2,1)S(1)}, u32[]{:S(2)}, u32[]{:S(2)}) collective-permute-start(bf16[16,3072]{1,0:T(8,128)(2,1)S(1)} %get-tuple-element.6), channel_id=1, source_target_pairs={{0,12},{4,28},{1,13},{5,29},{2,14},{6,30},{3,15},{7,31}} | collective-permute-start | bytes 294920 | tf_op jit(solution)/shard_map/ppermute | solution.py:257
  17.5 0.0 collective-permute-done.11.value_refs_1_
  17.5 0.0 copy-start.10
  17.5 0.7 %collective-permute-start = (bf16[16,3072]{1,0:T(8,128)(2,1)S(1)}, bf16[16,3072]{1,0:T(8,128)(2,1)S(1)}, u32[]{:S(2)}, u32[]{:S(2)}) collective-permute-start(bf16[16,3072]{1,0:T(8,128)(2,1)S(1)} %get-tuple-element.7), channel_id=1, source_target_pairs={{0,4},{4,20},{1,5},{5,21},{2,6},{6,22},{3,7},{7,23}} | collective-permute-start | bytes 294920 | tf_op jit(solution)/shard_map/ppermute | solution.py:257
  18.2 0.0 collective-permute-done.14.value_refs_4_
  18.2 0.0 copy-start.11
  18.2 0.1 collective-permute-start.9
  18.3 2.7 %collective-permute-done.3.first_refs_3_ = bf16[16,3072]{1,0:T(8,128)(2,1)S(1)} collective-permute-done((bf16[16,3072]{1,0:T(8,128)(2,1)S(1)}, bf16[16,3072]{1,0:T(8,128)(2,1)S(1)}, u32[]{:S(2)}, u32[]{:S(2)}) %collective-permute-start.3) | collective-permute-done | bytes 98336 | tf_op jit(solution)/shard_map/ppermute | solution.py:257
  21.0 1.9 %collective-permute-start.6 = (bf16[32,1024]{1,0:T(8,128)(2,1)S(1)}, bf16[32,1024]{1,0:T(8,128)(2,1)S(1)}, u32[]{:S(2)}, u32[]{:S(2)}) collective-permute-start(bf16[32,1024]{1,0:T(8,128)(2,1)S(1)} %collective-permute-done.5.key_refs_2_), channel_id=1, source_target_pairs={{16,20},{20,16},{24,28},{28,24},{17,21},{21,17},{25,29},{29,25},{1... | collective-permute-start | bytes 196616 | tf_op jit(solution)/shard_map/ppermute | solution.py:257
  22.9 0.0 collective-permute-done.2.first_refs_2_
  23.0 0.0 copy-start.1
  23.0 3.4 %collective-permute-start.13 = (bf16[32,1024]{1,0:T(8,128)(2,1)S(1)}, bf16[32,1024]{1,0:T(8,128)(2,1)S(1)}, u32[]{:S(2)}, u32[]{:S(2)}) collective-permute-start(bf16[32,1024]{1,0:T(8,128)(2,1)S(1)} %collective-permute-done.12.value_refs_2_), channel_id=1, source_target_pairs={{16,20},{20,16},{24,28},{28,24},{17,21},{21,17},{25,29},{29,25},{1... | collective-permute-start | bytes 196616 | tf_op jit(solution)/shard_map/ppermute | solution.py:257
  26.3 0.0 collective-permute-done.1.first_refs_1_
  26.3 0.0 copy-start.2
  26.4 0.1 collective-permute-start.16
  26.4 0.0 collective-permute-done.first_refs_0_
  26.4 0.0 copy-start.3
  26.5 0.5 %collective-permute-start.8 = (bf16[32,1024]{1,0:T(8,128)(2,1)S(1)}, bf16[32,1024]{1,0:T(8,128)(2,1)S(1)}, u32[]{:S(2)}, u32[]{:S(2)}) collective-permute-start(bf16[32,1024]{1,0:T(8,128)(2,1)S(1)} %collective-permute-done.4.key_refs_1_), channel_id=1, source_target_pairs={{0,8},{4,12},{8,0},{12,4},{16,24},{20,28},{24,16},{28,20},{1,9},{5... | collective-permute-start | bytes 196616 | tf_op jit(solution)/shard_map/ppermute | solution.py:257
  26.9 0.0 collective-permute-done.9.key_refs_6_
  26.9 0.1 collective-permute-start.15
  27.0 0.0 collective-permute-done.6.key_refs_3_
  27.0 0.4 %collective-permute-start.10 = (bf16[32,1024]{1,0:T(8,128)(2,1)S(1)}, bf16[32,1024]{1,0:T(8,128)(2,1)S(1)}, u32[]{:S(2)}, u32[]{:S(2)}) collective-permute-start(bf16[32,1024]{1,0:T(8,128)(2,1)S(1)} %collective-permute-done.6.key_refs_3_), channel_id=1, source_target_pairs={{0,8},{4,12},{8,0},{12,4},{16,24},{20,28},{24,16},{28,20},{1,9},{5... | collective-permute-start | bytes 196616 | tf_op jit(solution)/shard_map/ppermute | solution.py:257
  27.5 1.0 %collective-permute-done.13.value_refs_3_ = bf16[32,1024]{1,0:T(8,128)(2,1)S(1)} collective-permute-done((bf16[32,1024]{1,0:T(8,128)(2,1)S(1)}, bf16[32,1024]{1,0:T(8,128)(2,1)S(1)}, u32[]{:S(2)}, u32[]{:S(2)}) %collective-permute-start.13) | collective-permute-done | bytes 65568 | tf_op jit(solution)/shard_map/ppermute | solution.py:257
  28.4 0.9 %collective-permute-start.17 = (bf16[32,1024]{1,0:T(8,128)(2,1)S(1)}, bf16[32,1024]{1,0:T(8,128)(2,1)S(1)}, u32[]{:S(2)}, u32[]{:S(2)}) collective-permute-start(bf16[32,1024]{1,0:T(8,128)(2,1)S(1)} %collective-permute-done.13.value_refs_3_), channel_id=1, source_target_pairs={{0,8},{4,12},{8,0},{12,4},{16,24},{20,28},{24,16},{28,20},{1,9},{5... | collective-permute-start | bytes 196616 | tf_op jit(solution)/shard_map/ppermute | solution.py:257
  29.4 0.0 collective-permute-done.8.key_refs_5_
  29.4 0.0 collective-permute-done.16.value_refs_6_
  29.4 0.0 copy-start.15
  29.4 0.0 collective-permute-done.15.value_refs_5_
  29.4 0.0 copy-start.17
  29.4 0.0 collective-permute-done.10.key_refs_7_
  29.4 0.0 copy-start.18
  29.4 0.8 %collective-permute-done.17.value_refs_7_ = bf16[32,1024]{1,0:T(8,128)(2,1)S(1)} collective-permute-done((bf16[32,1024]{1,0:T(8,128)(2,1)S(1)}, bf16[32,1024]{1,0:T(8,128)(2,1)S(1)}, u32[]{:S(2)}, u32[]{:S(2)}) %collective-permute-start.17) | collective-permute-done | bytes 65568 | tf_op jit(solution)/shard_map/ppermute | solution.py:257
  30.3 0.0 copy-done.6
  30.3 0.0 copy-done.7
  30.3 0.0 copy-done.8
  30.3 0.0 copy-done.9
  30.3 0.0 copy-done.10
  30.4 0.5 %copy-done.19 = bf16[32,1024]{1,0:T(8,128)(2,1)} copy-done((bf16[32,1024]{1,0:T(8,128)(2,1)}, bf16[32,1024]{1,0:T(8,128)(2,1)S(1)}, u32[]{:S(2)}) %copy-start.19) | copy-done | bytes 65560
  30.9 3.6 %attention.1 = (bf16[32,6144]{1,0:T(8,128)(2,1)}, bf16[16,3072]{1,0:T(8,128)(2,1)}) custom-call(s32[4]{0:T(128)} %counts_ref.1, s32[4,4]{1,0:T(4,128)} %visible_ref.1, bf16[32,6144]{1,0:T(8,128)(2,1)} %query_ref.1, bf16[16,3072]{1,0:T(8,128)(2,1)} %copy-done.3, bf16[16,3072]{1,0:T(8,128)(2,1)} %copy-done.2, bf16[16,3072]{1,0:T(8,128)(2,1)} %copy-done.1, ...), custom_call_target="tpu_custom_call" | custom-call | tf_op jit(solution)/shard_map/attention/pallas_call | solution.py:283
  (22 shorter events, 0.0 us)
Async XLA Ops:
  0.6 8.0 %copy-start.4 = (bf16[32,1024]{1,0:T(8,128)(2,1)S(1)}, bf16[32,1024]{1,0:T(8,128)(2,1)}, u32[]{:S(2)}) copy-start(bf16[32,1024]{1,0:T(8,128)(2,1)} %key_refs_0_.1) | copy-start | bytes 196612
  7.4 6.7 %copy-start.20 = (f32[1,3072]{1,0:T(1,128)}, f32[1,3072]{1,0:T(1,128)S(1)}, u32[]{:S(2)}) copy-start(f32[1,3072]{1,0:T(1,128)S(1)} %get-tuple-element.3.gain_ref) | copy-start | bytes 36868
  7.4 8.8 %copy-start.5 = (bf16[32,1024]{1,0:T(8,128)(2,1)S(1)}, bf16[32,1024]{1,0:T(8,128)(2,1)}, u32[]{:S(2)}) copy-start(bf16[32,1024]{1,0:T(8,128)(2,1)} %value_refs_0_.1) | copy-start | bytes 196612
  7.4 4.5 %collective-permute-start.18 = (f32[1,3072]{1,0:T(1,128)S(1)}, f32[1,3072]{1,0:T(1,128)S(1)}, u32[]{:S(2)}, u32[]{:S(2)}) collective-permute-start(f32[1,3072]{1,0:T(1,128)S(1)} %get-tuple-element.3.gain_ref), channel_id=1, source_target_pairs={{0,4},{4,0},{8,12},{12,8},{16,20},{20,16},{24,28},{28,24},{1,5},{5... | collective-permute-start | bytes 36872 | tf_op jit(solution)/shard_map/ppermute | solution.py:257
  8.6 5.5 %collective-permute-start.5 = (bf16[32,1024]{1,0:T(8,128)(2,1)S(1)}, bf16[32,1024]{1,0:T(8,128)(2,1)S(1)}, u32[]{:S(2)}, u32[]{:S(2)}) collective-permute-start(bf16[32,1024]{1,0:T(8,128)(2,1)S(1)} %copy-done.4), channel_id=1, source_target_pairs={{0,16},{4,20},{8,24},{12,28},{16,0},{20,4},{24,8},{28,12},{1,17},{... | collective-permute-start | bytes 196616 | tf_op jit(solution)/shard_map/ppermute | solution.py:257
  8.9 6.6 %collective-permute-start.4 = (bf16[32,1024]{1,0:T(8,128)(2,1)S(1)}, bf16[32,1024]{1,0:T(8,128)(2,1)S(1)}, u32[]{:S(2)}, u32[]{:S(2)}) collective-permute-start(bf16[32,1024]{1,0:T(8,128)(2,1)S(1)} %copy-done.4), channel_id=1, source_target_pairs={{0,4},{4,0},{8,12},{12,8},{16,20},{20,16},{24,28},{28,24},{1,5},{5... | collective-permute-start | bytes 196616 | tf_op jit(solution)/shard_map/ppermute | solution.py:257
  9.1 7.1 %collective-permute-start.7 = (bf16[32,1024]{1,0:T(8,128)(2,1)S(1)}, bf16[32,1024]{1,0:T(8,128)(2,1)S(1)}, u32[]{:S(2)}, u32[]{:S(2)}) collective-permute-start(bf16[32,1024]{1,0:T(8,128)(2,1)S(1)} %copy-done.4), channel_id=1, source_target_pairs={{0,8},{4,12},{8,0},{12,4},{16,24},{20,28},{24,16},{28,20},{1,9},{5... | collective-permute-start | bytes 196616 | tf_op jit(solution)/shard_map/ppermute | solution.py:257
  10.7 6.2 %collective-permute-start.12 = (bf16[32,1024]{1,0:T(8,128)(2,1)}, bf16[32,1024]{1,0:T(8,128)(2,1)S(1)}, u32[]{:S(2)}, u32[]{:S(2)}) collective-permute-start(bf16[32,1024]{1,0:T(8,128)(2,1)} %value_refs_0_.1), channel_id=1, source_target_pairs={{0,16},{4,20},{8,24},{12,28},{16,0},{20,4},{24,8},{28,12},{1,17},{... | collective-permute-start | bytes 196616 | tf_op jit(solution)/shard_map/ppermute | solution.py:257
  11.9 2.3 %copy-start.21 = (f32[1,3072]{1,0:T(1,128)}, f32[1,3072]{1,0:T(1,128)S(1)}, u32[]{:S(2)}) copy-start(f32[1,3072]{1,0:T(1,128)S(1)} %collective-permute-done.18.far_gain_ref) | copy-start | bytes 36868
  11.9 5.6 %collective-permute-start.11 = (bf16[32,1024]{1,0:T(8,128)(2,1)}, bf16[32,1024]{1,0:T(8,128)(2,1)S(1)}, u32[]{:S(2)}, u32[]{:S(2)}) collective-permute-start(bf16[32,1024]{1,0:T(8,128)(2,1)} %value_refs_0_.1), channel_id=1, source_target_pairs={{0,4},{4,0},{8,12},{12,8},{16,20},{20,16},{24,28},{28,24},{1,5},{5... | collective-permute-start | bytes 196616 | tf_op jit(solution)/shard_map/ppermute | solution.py:257
  14.2 16.1 %copy-start.6 = (bf16[32,1024]{1,0:T(8,128)(2,1)}, bf16[32,1024]{1,0:T(8,128)(2,1)S(1)}, u32[]{:S(2)}) copy-start(bf16[32,1024]{1,0:T(8,128)(2,1)S(1)} %collective-permute-done.5.key_refs_2_) | copy-start | bytes 196612
  14.2 6.8 %collective-permute-start.3 = (bf16[16,3072]{1,0:T(8,128)(2,1)S(1)}, bf16[16,3072]{1,0:T(8,128)(2,1)S(1)}, u32[]{:S(2)}, u32[]{:S(2)}) collective-permute-start(bf16[16,3072]{1,0:T(8,128)(2,1)S(1)} %get-tuple-element.4), channel_id=1, source_target_pairs={{0,8},{4,24},{1,9},{5,25},{2,10},{6,26},{3,11},{7,27}} | collective-permute-start | bytes 294920 | tf_op jit(solution)/shard_map/ppermute | solution.py:257
  15.5 14.8 %copy-start.7 = (bf16[32,1024]{1,0:T(8,128)(2,1)}, bf16[32,1024]{1,0:T(8,128)(2,1)S(1)}, u32[]{:S(2)}) copy-start(bf16[32,1024]{1,0:T(8,128)(2,1)S(1)} %collective-permute-done.4.key_refs_1_) | copy-start | bytes 196612
  15.5 7.4 %collective-permute-start.2 = (bf16[16,3072]{1,0:T(8,128)(2,1)S(1)}, bf16[16,3072]{1,0:T(8,128)(2,1)S(1)}, u32[]{:S(2)}, u32[]{:S(2)}) collective-permute-start(bf16[16,3072]{1,0:T(8,128)(2,1)S(1)} %get-tuple-element.5), channel_id=1, source_target_pairs={{4,16},{5,17},{6,18},{7,19}} | collective-permute-start | bytes 294920 | tf_op jit(solution)/shard_map/ppermute | solution.py:257
  16.2 14.1 %copy-start.8 = (bf16[32,1024]{1,0:T(8,128)(2,1)}, bf16[32,1024]{1,0:T(8,128)(2,1)S(1)}, u32[]{:S(2)}) copy-start(bf16[32,1024]{1,0:T(8,128)(2,1)S(1)} %collective-permute-done.7.key_refs_4_) | copy-start | bytes 196612
  16.2 2.0 %collective-permute-start.14 = (bf16[32,1024]{1,0:T(8,128)(2,1)S(1)}, bf16[32,1024]{1,0:T(8,128)(2,1)S(1)}, u32[]{:S(2)}, u32[]{:S(2)}) collective-permute-start(bf16[32,1024]{1,0:T(8,128)(2,1)S(1)} %copy-done.5), channel_id=1, source_target_pairs={{0,8},{4,12},{8,0},{12,4},{16,24},{20,28},{24,16},{28,20},{1,9},{5... | collective-permute-start | bytes 196616 | tf_op jit(solution)/shard_map/ppermute | solution.py:257
  16.8 13.4 %copy-start.9 = (bf16[32,1024]{1,0:T(8,128)(2,1)}, bf16[32,1024]{1,0:T(8,128)(2,1)S(1)}, u32[]{:S(2)}) copy-start(bf16[32,1024]{1,0:T(8,128)(2,1)S(1)} %collective-permute-done.12.value_refs_2_) | copy-start | bytes 196612
  16.8 9.5 %collective-permute-start.1 = (bf16[16,3072]{1,0:T(8,128)(2,1)S(1)}, bf16[16,3072]{1,0:T(8,128)(2,1)S(1)}, u32[]{:S(2)}, u32[]{:S(2)}) collective-permute-start(bf16[16,3072]{1,0:T(8,128)(2,1)S(1)} %get-tuple-element.6), channel_id=1, source_target_pairs={{0,12},{4,28},{1,13},{5,29},{2,14},{6,30},{3,15},{7,31}} | collective-permute-start | bytes 294920 | tf_op jit(solution)/shard_map/ppermute | solution.py:257
  17.5 12.8 %copy-start.10 = (bf16[32,1024]{1,0:T(8,128)(2,1)}, bf16[32,1024]{1,0:T(8,128)(2,1)S(1)}, u32[]{:S(2)}) copy-start(bf16[32,1024]{1,0:T(8,128)(2,1)S(1)} %collective-permute-done.11.value_refs_1_) | copy-start | bytes 196612
  17.5 8.9 %collective-permute-start = (bf16[16,3072]{1,0:T(8,128)(2,1)S(1)}, bf16[16,3072]{1,0:T(8,128)(2,1)S(1)}, u32[]{:S(2)}, u32[]{:S(2)}) collective-permute-start(bf16[16,3072]{1,0:T(8,128)(2,1)S(1)} %get-tuple-element.7), channel_id=1, source_target_pairs={{0,4},{4,20},{1,5},{5,21},{2,6},{6,22},{3,7},{7,23}} | collective-permute-start | bytes 294920 | tf_op jit(solution)/shard_map/ppermute | solution.py:257
  18.2 12.1 %copy-start.11 = (bf16[32,1024]{1,0:T(8,128)(2,1)}, bf16[32,1024]{1,0:T(8,128)(2,1)S(1)}, u32[]{:S(2)}) copy-start(bf16[32,1024]{1,0:T(8,128)(2,1)S(1)} %collective-permute-done.14.value_refs_4_) | copy-start | bytes 196612
  18.2 8.7 %collective-permute-start.9 = (bf16[32,1024]{1,0:T(8,128)(2,1)S(1)}, bf16[32,1024]{1,0:T(8,128)(2,1)S(1)}, u32[]{:S(2)}, u32[]{:S(2)}) collective-permute-start(bf16[32,1024]{1,0:T(8,128)(2,1)S(1)} %collective-permute-done.5.key_refs_2_), channel_id=1, source_target_pairs={{0,8},{4,12},{8,0},{12,4},{16,24},{20,28},{24,16},{28,20},{1,9},{5... | collective-permute-start | bytes 196616 | tf_op jit(solution)/shard_map/ppermute | solution.py:257
  21.0 9.3 %copy-start = (bf16[16,3072]{1,0:T(8,128)(2,1)}, bf16[16,3072]{1,0:T(8,128)(2,1)S(1)}, u32[]{:S(2)}) copy-start(bf16[16,3072]{1,0:T(8,128)(2,1)S(1)} %collective-permute-done.3.first_refs_3_) | copy-start | bytes 294916
  21.0 6.0 %collective-permute-start.6 = (bf16[32,1024]{1,0:T(8,128)(2,1)S(1)}, bf16[32,1024]{1,0:T(8,128)(2,1)S(1)}, u32[]{:S(2)}, u32[]{:S(2)}) collective-permute-start(bf16[32,1024]{1,0:T(8,128)(2,1)S(1)} %collective-permute-done.5.key_refs_2_), channel_id=1, source_target_pairs={{16,20},{20,16},{24,28},{28,24},{17,21},{21,17},{25,29},{29,25},{1... | collective-permute-start | bytes 196616 | tf_op jit(solution)/shard_map/ppermute | solution.py:257
  23.0 7.4 %copy-start.1 = (bf16[16,3072]{1,0:T(8,128)(2,1)}, bf16[16,3072]{1,0:T(8,128)(2,1)S(1)}, u32[]{:S(2)}) copy-start(bf16[16,3072]{1,0:T(8,128)(2,1)S(1)} %collective-permute-done.2.first_refs_2_) | copy-start | bytes 294916
  23.0 5.5 %collective-permute-start.13 = (bf16[32,1024]{1,0:T(8,128)(2,1)S(1)}, bf16[32,1024]{1,0:T(8,128)(2,1)S(1)}, u32[]{:S(2)}, u32[]{:S(2)}) collective-permute-start(bf16[32,1024]{1,0:T(8,128)(2,1)S(1)} %collective-permute-done.12.value_refs_2_), channel_id=1, source_target_pairs={{16,20},{20,16},{24,28},{28,24},{17,21},{21,17},{25,29},{29,25},{1... | collective-permute-start | bytes 196616 | tf_op jit(solution)/shard_map/ppermute | solution.py:257
  26.3 4.0 %copy-start.2 = (bf16[16,3072]{1,0:T(8,128)(2,1)}, bf16[16,3072]{1,0:T(8,128)(2,1)S(1)}, u32[]{:S(2)}) copy-start(bf16[16,3072]{1,0:T(8,128)(2,1)S(1)} %collective-permute-done.1.first_refs_1_) | copy-start | bytes 294916
  26.4 3.0 %collective-permute-start.16 = (bf16[32,1024]{1,0:T(8,128)(2,1)S(1)}, bf16[32,1024]{1,0:T(8,128)(2,1)S(1)}, u32[]{:S(2)}, u32[]{:S(2)}) collective-permute-start(bf16[32,1024]{1,0:T(8,128)(2,1)S(1)} %collective-permute-done.12.value_refs_2_), channel_id=1, source_target_pairs={{0,8},{4,12},{8,0},{12,4},{16,24},{20,28},{24,16},{28,20},{1,9},{5... | collective-permute-start | bytes 196616 | tf_op jit(solution)/shard_map/ppermute | solution.py:257
  26.4 3.9 %copy-start.3 = (bf16[16,3072]{1,0:T(8,128)(2,1)}, bf16[16,3072]{1,0:T(8,128)(2,1)S(1)}, u32[]{:S(2)}) copy-start(bf16[16,3072]{1,0:T(8,128)(2,1)S(1)} %collective-permute-done.first_refs_0_) | copy-start | bytes 294916
  26.5 2.9 %collective-permute-start.8 = (bf16[32,1024]{1,0:T(8,128)(2,1)S(1)}, bf16[32,1024]{1,0:T(8,128)(2,1)S(1)}, u32[]{:S(2)}, u32[]{:S(2)}) collective-permute-start(bf16[32,1024]{1,0:T(8,128)(2,1)S(1)} %collective-permute-done.4.key_refs_1_), channel_id=1, source_target_pairs={{0,8},{4,12},{8,0},{12,4},{16,24},{20,28},{24,16},{28,20},{1,9},{5... | collective-permute-start | bytes 196616 | tf_op jit(solution)/shard_map/ppermute | solution.py:257
  26.9 3.4 %copy-start.12 = (bf16[32,1024]{1,0:T(8,128)(2,1)}, bf16[32,1024]{1,0:T(8,128)(2,1)S(1)}, u32[]{:S(2)}) copy-start(bf16[32,1024]{1,0:T(8,128)(2,1)S(1)} %collective-permute-done.9.key_refs_6_) | copy-start | bytes 196612
  26.9 2.5 %collective-permute-start.15 = (bf16[32,1024]{1,0:T(8,128)(2,1)S(1)}, bf16[32,1024]{1,0:T(8,128)(2,1)S(1)}, u32[]{:S(2)}, u32[]{:S(2)}) collective-permute-start(bf16[32,1024]{1,0:T(8,128)(2,1)S(1)} %collective-permute-done.11.value_refs_1_), channel_id=1, source_target_pairs={{0,8},{4,12},{8,0},{12,4},{16,24},{20,28},{24,16},{28,20},{1,9},{5... | collective-permute-start | bytes 196616 | tf_op jit(solution)/shard_map/ppermute | solution.py:257
  27.0 3.3 %copy-start.13 = (bf16[32,1024]{1,0:T(8,128)(2,1)}, bf16[32,1024]{1,0:T(8,128)(2,1)S(1)}, u32[]{:S(2)}) copy-start(bf16[32,1024]{1,0:T(8,128)(2,1)S(1)} %collective-permute-done.6.key_refs_3_) | copy-start | bytes 196612
  27.0 2.4 %collective-permute-start.10 = (bf16[32,1024]{1,0:T(8,128)(2,1)S(1)}, bf16[32,1024]{1,0:T(8,128)(2,1)S(1)}, u32[]{:S(2)}, u32[]{:S(2)}) collective-permute-start(bf16[32,1024]{1,0:T(8,128)(2,1)S(1)} %collective-permute-done.6.key_refs_3_), channel_id=1, source_target_pairs={{0,8},{4,12},{8,0},{12,4},{16,24},{20,28},{24,16},{28,20},{1,9},{5... | collective-permute-start | bytes 196616 | tf_op jit(solution)/shard_map/ppermute | solution.py:257
  28.4 1.9 %copy-start.14 = (bf16[32,1024]{1,0:T(8,128)(2,1)}, bf16[32,1024]{1,0:T(8,128)(2,1)S(1)}, u32[]{:S(2)}) copy-start(bf16[32,1024]{1,0:T(8,128)(2,1)S(1)} %collective-permute-done.13.value_refs_3_) | copy-start | bytes 196612
  28.4 1.8 %collective-permute-start.17 = (bf16[32,1024]{1,0:T(8,128)(2,1)S(1)}, bf16[32,1024]{1,0:T(8,128)(2,1)S(1)}, u32[]{:S(2)}, u32[]{:S(2)}) collective-permute-start(bf16[32,1024]{1,0:T(8,128)(2,1)S(1)} %collective-permute-done.13.value_refs_3_), channel_id=1, source_target_pairs={{0,8},{4,12},{8,0},{12,4},{16,24},{20,28},{24,16},{28,20},{1,9},{5... | collective-permute-start | bytes 196616 | tf_op jit(solution)/shard_map/ppermute | solution.py:257
  29.4 1.0 %copy-start.16 = (bf16[32,1024]{1,0:T(8,128)(2,1)}, bf16[32,1024]{1,0:T(8,128)(2,1)S(1)}, u32[]{:S(2)}) copy-start(bf16[32,1024]{1,0:T(8,128)(2,1)S(1)} %collective-permute-done.8.key_refs_5_) | copy-start | bytes 196612
  29.4 1.0 %copy-start.15 = (bf16[32,1024]{1,0:T(8,128)(2,1)}, bf16[32,1024]{1,0:T(8,128)(2,1)S(1)}, u32[]{:S(2)}) copy-start(bf16[32,1024]{1,0:T(8,128)(2,1)S(1)} %collective-permute-done.16.value_refs_6_) | copy-start | bytes 196612
  29.4 1.0 %copy-start.17 = (bf16[32,1024]{1,0:T(8,128)(2,1)}, bf16[32,1024]{1,0:T(8,128)(2,1)S(1)}, u32[]{:S(2)}) copy-start(bf16[32,1024]{1,0:T(8,128)(2,1)S(1)} %collective-permute-done.15.value_refs_5_) | copy-start | bytes 196612
  29.4 1.0 %copy-start.18 = (bf16[32,1024]{1,0:T(8,128)(2,1)}, bf16[32,1024]{1,0:T(8,128)(2,1)S(1)}, u32[]{:S(2)}) copy-start(bf16[32,1024]{1,0:T(8,128)(2,1)S(1)} %collective-permute-done.10.key_refs_7_) | copy-start | bytes 196612
  30.3 0.6 %copy-start.19 = (bf16[32,1024]{1,0:T(8,128)(2,1)}, bf16[32,1024]{1,0:T(8,128)(2,1)S(1)}, u32[]{:S(2)}) copy-start(bf16[32,1024]{1,0:T(8,128)(2,1)S(1)} %collective-permute-done.17.value_refs_7_) | copy-start | bytes 196612

commit v2 on v0

--- a/solution.py
+++ b/solution.py
@@ -3,6 +3,8 @@
 import jax
 import jax.numpy as jnp
 from jax import lax
+from jax.experimental import pallas as pl
+from jax.experimental.pallas import tpu as pltpu
 from jax.sharding import PartitionSpec as P
 
 QUERY_HEADS = 48
@@ -18,7 +20,7 @@
     return lax.ppermute(block, axis, route)
 
 
-def body(queries, keys, values, level_gain, levels, visible, counts):
+def general_body(queries, keys, values, level_gain, levels, visible, counts):
     head_count = lax.axis_size("head")
     ctx_count = lax.axis_size("ctx")
     ctx_index = lax.axis_index("ctx")
@@ -153,6 +155,163 @@
     return (mixed, finished)
 
 
+KERNEL_BYTES = 8 << 20
+
+
+def prepare_kernel(levels_ref, visible_ref, counts_ref, gain_ref, gains_ref, bias_ref, live_ref):
+    ctx, head = lax.axis_index("ctx"), lax.axis_index("head")
+    for place, clip in enumerate((ctx, 0)):
+        gains_ref[pl.ds(place, 1)] = gain_ref[pl.ds(levels_ref[clip], 1)]
+    key_count = bias_ref.shape[1]
+    rows = live_ref.shape[1]
+    first_rows = rows * 2 // CLIPS
+
+    lane = lax.broadcasted_iota(jnp.int32, (1, key_count), 1)
+    piece = lane // rows
+    place = jnp.where(piece % 2 == head, 0, rows) + lane % rows
+    bias = jnp.full((1, key_count), -1e30, jnp.float32)
+    first_bias = bias
+    for flip in range(CLIPS):
+        clip = ctx ^ ((flip % 2) * 2) ^ (flip // 2)
+        here = (piece // 2 == flip) & (place < counts_ref[clip])
+        seen = jnp.where(visible_ref[ctx, clip] == 1, 0.0, -1e30)
+        bias = jnp.where(here, seen, bias)
+        first_bias = jnp.where(here, jnp.where(clip == 0, 0.0, -1e30), first_bias)
+    bias_ref[:1] = bias
+    bias_ref[1:] = first_bias
+    row = lax.broadcasted_iota(jnp.int32, live_ref.shape[1:], 0)
+    live_ref[0] = jnp.where(row + head * rows < counts_ref[ctx], 1.0, 0.0)
+    live_ref[1] = jnp.where(row + ctx * first_rows < counts_ref[0], 1.0, 0.0)
+
+
+def attend(query_pieces, keys, values, key_bias):
+    scale = 1.0 / math.sqrt(HEAD_SIZE)
+    stacked = jnp.concatenate(query_pieces, axis=0)
+    scores = lax.dot_general(
+        stacked, keys, (((1,), (1,)), ((), ())), preferred_element_type=jnp.float32
+    )
+    scores = scores * scale + key_bias
+    peak = jnp.max(scores, axis=1, keepdims=True)
+    probs = jnp.exp(scores - peak)
+    denominator = jnp.sum(probs, axis=1, keepdims=True)
+    weighted = jnp.dot(probs.astype(jnp.bfloat16), values, preferred_element_type=jnp.float32)
+    return weighted / denominator
+
+
+def attention_kernel(query_ref, key_refs, value_refs, bias_ref, live_ref, gain_ref, far_gain_ref, mixed_ref):
+    head = lax.axis_index("head")
+    rows, width = query_ref.shape
+    half = width // 2
+    group = QUERY_HEADS // KEY_VALUE_HEADS
+    live = live_ref[0] != 0.0
+    for kv_head in range(KEY_VALUE_HEADS):
+        columns = slice(kv_head * HEAD_SIZE, (kv_head + 1) * HEAD_SIZE)
+        keys = jnp.concatenate([ref[:, columns] for ref in key_refs], axis=0)
+        values = jnp.concatenate([ref[:, columns] for ref in value_refs], axis=0)
+        start = kv_head * group * HEAD_SIZE
+        spans = [slice(start + g * HEAD_SIZE, start + (g + 1) * HEAD_SIZE) for g in range(group)]
+        attended = attend([query_ref[:, span] for span in spans], keys, values, bias_ref[:1])
+        for g, span in enumerate(spans):
+            side = span.start // half
+            local = slice(span.start - side * half, span.stop - side * half)
+            gain = jnp.where(head == side, gain_ref[:1, local], far_gain_ref[:1, local])
+            block = attended[g * rows : (g + 1) * rows] * gain
+            mixed_ref[:, span] = jnp.where(live, block, 0.0).astype(mixed_ref.dtype)
+
+
+def first_kernel(query_refs, key_refs, value_refs, bias_ref, live_ref, gain_ref, finished_ref):
+    ctx, head = lax.axis_index("ctx"), lax.axis_index("head")
+    kept_ref, beside_ref, across_ref = query_refs
+    rows = finished_ref.shape[0]
+    group = QUERY_HEADS // KEY_VALUE_HEADS
+    live = live_ref[1, :rows] != 0.0
+    for kv_head in range(KEY_VALUE_HEADS // 2):
+        start = pl.multiple_of((head * (KEY_VALUE_HEADS // 2) + kv_head) * HEAD_SIZE, HEAD_SIZE)
+        columns = pl.ds(start, HEAD_SIZE)
+        keys = jnp.concatenate([ref[:, columns] for ref in key_refs], axis=0)
+        values = jnp.concatenate([ref[:, columns] for ref in value_refs], axis=0)
+        start = kv_head * group * HEAD_SIZE
+        spans = [slice(start + g * HEAD_SIZE, start + (g + 1) * HEAD_SIZE) for g in range(group)]
+        query_pieces = [
+            jnp.where(
+                ctx < 2,
+                jnp.where(head == 0, kept_ref[:, span], beside_ref[:, span]),
+                across_ref[:, span],
+            )
+            for span in spans
+        ]
+        attended = attend(query_pieces, keys, values, bias_ref[1:])
+        for g, span in enumerate(spans):
+            block = attended[g * rows : (g + 1) * rows] * gain_ref[1:, span]
+            finished_ref[:, span] = jnp.where(live, block, 0.0).astype(finished_ref.dtype)
+
+
+def paired_body(queries, keys, values, level_gain, levels, visible, counts):
+    axes = ("ctx", "head")
+    places = [(c, h) for c in range(CLIPS) for h in range(2)]
+    ctx, head = lax.axis_index("ctx"), lax.axis_index("head")
+    rows, width = queries.shape
+    half = width // 2
+    first_rows = rows * 2 // CLIPS
+
+    def move(block, route):
+        pairs = [(a * 2 + b, c * 2 + d) for (a, b), (c, d) in route]
+        return lax.ppermute(block, axes, pairs)
+
+    beside = [((c, h), (c, 1 - h)) for c, h in places]
+    across = [((c, h), (c ^ 2, h)) for c, h in places]
+    partner = [((c, h), (c ^ 1, h)) for c, h in places]
+    smem, vmem = pl.BlockSpec(memory_space=pltpu.SMEM), pl.BlockSpec(memory_space=pltpu.VMEM)
+    params = pltpu.CompilerParams(vmem_limit_bytes=KERNEL_BYTES)
+    swapped = move(queries, partner)
+    beside_keys, beside_values = move(keys, beside), move(values, beside)
+    across_keys, across_values = move(keys, across), move(values, across)
+    relay_keys, relay_values = move(beside_keys, across), move(beside_values, across)
+    near_keys = [keys, beside_keys, across_keys, relay_keys]
+    near_values = [values, beside_values, across_values, relay_values]
+    all_keys = near_keys + [move(b, partner) for b in near_keys]
+    all_values = near_values + [move(b, partner) for b in near_values]
+
+    mine = jnp.where(ctx % 2 == 0, queries[:first_rows], swapped[first_rows:])
+    left, right = mine[:, :half], mine[:, half:]
+    sent, kept = jnp.where(head == 0, right, left), jnp.where(head == 0, left, right)
+    first_beside = move(sent, beside)
+    onward = jnp.where(head == 1, kept, first_beside)
+    first_across = move(onward, across)
+
+    gains, bias, live = pl.pallas_call(
+        prepare_kernel,
+        out_shape=(
+            jax.ShapeDtypeStruct((2, half), level_gain.dtype),
+            jax.ShapeDtypeStruct((2, len(all_keys) * rows), jnp.float32),
+            jax.ShapeDtypeStruct((2, rows, HEAD_SIZE), jnp.float32),
+        ),
+        in_specs=[smem, smem, smem, vmem],
+        out_specs=(vmem, vmem, vmem),
+        compiler_params=params,
+        name="prepare",
+    )(levels, visible, counts, level_gain)
+    far_gains = move(gains, beside)
+    pieces = [vmem] * len(all_keys)
+    mixed = pl.pallas_call(
+        attention_kernel,
+        out_shape=jax.ShapeDtypeStruct((rows, width), queries.dtype),
+        in_specs=[vmem, pieces, pieces, vmem, vmem, vmem, vmem],
+        out_specs=vmem,
+        compiler_params=params,
+        name="attention",
+    )(queries, all_keys, all_values, bias, live, gains, far_gains)
+    finished = pl.pallas_call(
+        first_kernel,
+        out_shape=jax.ShapeDtypeStruct((first_rows, half), queries.dtype),
+        in_specs=[[vmem] * 3, pieces, pieces, vmem, vmem, vmem],
+        out_specs=vmem,
+        compiler_params=params,
+        name="first_clip",
+    )([kept, first_beside, first_across], all_keys, all_values, bias, live, gains)
+    return mixed, finished
+
+
 def solution(mesh):
     placed = (
         P(("dp", "ctx", "head"), None),
@@ -163,8 +322,10 @@
         P("dp", None),
         P("dp"),
     )
+    axes = mesh.shape
+    paired = axes["ctx"] == CLIPS and axes["head"] == 2
     return jax.shard_map(
-        body,
+        paired_body if paired else general_body,
         mesh=mesh,
         in_specs=placed,
         out_specs=(P(("dp", "ctx", "head"), None), P(("dp", "ctx"), "head")),

time: 62.2 us -> 25.6 us (0.41); the launches traced: 61.5 us -> 25.5 us
  blocking collectives: 12.1 us -> 0 us
  local copies, waits for them, and re-layouts: 9.12 us -> 0.04 us
  starting transfers between devices: 21.2 us -> 15.3 us
  matrix products: 4.5 us -> 0 us
  Pallas kernels: 0 us -> 3.94 us
  other arithmetic: 4.82 us -> 0.99 us
  waiting for transfers between devices: 8.19 us -> 4.46 us
  between operations: 1.43 us -> 0.74 us
    all_to_all x4 -> x0, starting transfers between devices: 14.5 us -> none  [the longest x1 4.23 us: body(): lax.all_to_all(keys, 'head', split_axis=1, concat_axis=0, tiled=True)]
    all_gather x2 -> x0, blocking collectives: 12.1 us -> none  [the longest x1 6.31 us: body(): key_piece = lax.all_gather(key_local, 'ctx', axis=0, tiled=True)]
    ppermute x3 -> x18, starting transfers between devices: 6.7 us -> 15.3 us  [move(): return lax.ppermute(block, axes, pairs)]
    all_to_all x4 -> x0, waiting for transfers between devices: 8.18 us -> none  [the longest x1 6.56 us: body(): lax.all_to_all(gated, 'head', split_axis=0, concat_axis=1, tiled=True)]
    all_to_all x4 -> x0, local copies, waits for them, and re-layouts: 5.55 us -> none  [the longest x1 1.77 us: body(): lax.all_to_all(queries, 'head', split_axis=1, concat_axis=0, tiled=True)]
    dot_general x3 -> x0, matrix products: 4.5 us -> none  [the longest x1 1.63 us: update(): jnp.einsum('rkgd,nkd->rkgn', query_grouped, key_head_rows, preferred_elem...]
    ppermute x3 -> x18, waiting for transfers between devices: 0.01 us -> 4.46 us  [move(): return lax.ppermute(block, axes, pairs)]
    pallas_call x0 -> x3, Pallas kernels: none -> 3.94 us  [the longest x1 1.78 us: paired_body(): pl.pallas_call(attention_kernel, out_shape=jax.ShapeDtypeStruct((rows, wi...]
  transfers between devices with their start and end apart: 7 -> 18, of which waited for: 2 -> 7; matrix products, arithmetic and copies ran while one was open for 12% -> 4% of each run, Pallas kernels for 0% -> 9%
where the time goes in v2:
time: 25.6 us; the launch traced here: 25.5 us
  starting transfers between devices  15.3 us (60%)
  waiting for transfers between devices  4.46 us (17%)
  Pallas kernels  3.94 us (15%)
  other arithmetic  0.99 us (4%)
  between operations  0.74 us (3%)
    ppermute x18, starting transfers between devices, move(): return lax.ppermute(block, axes, pairs)  15.3 us
    ppermute x18, waiting for transfers between devices, move(): return lax.ppermute(block, axes, pairs)  4.46 us
    pallas_call x1, Pallas kernels, paired_body(): pl.pallas_call(attention_kernel, out_shape=jax.ShapeDtypeStruct((rows, wi...  1.78 us
    pallas_call x1, Pallas kernels, paired_body(): pl.pallas_call(first_kernel, out_shape=jax.ShapeDtypeStruct((first_rows,...  1.55 us
    select_n x1, other arithmetic, paired_body(): mine = jnp.where(ctx % 2 == 0, queries[:first_rows], swapped[first_rows:])  0.95 us
    pallas_call x1, Pallas kernels, paired_body(): pl.pallas_call(prepare_kernel, out_shape=(jax.ShapeDtypeStruct((2, half),...  0.61 us
  transfers between devices with their start and end apart: 18, of which 7 were waited for; matrix products, arithmetic and copies ran while one was open for 4% of the time, Pallas kernels for 9%

profile of v2, /device:TPU:0, one launch (start us, length us, event | category | flops | bytes accessed | tf_op | source)
XLA Modules:
  0.0 25.5 jit_solution(17652440205668437863)
XLA Ops:
  0.6 0.0 copy-start.1
  0.6 0.6 %collective-permute-start.15 = (bf16[32,6144]{1,0:T(8,128)(2,1)}, bf16[32,6144]{1,0:T(8,128)(2,1)S(1)}, u32[]{:S(2)}, u32[]{:S(2)}) collective-permute-start(bf16[32,6144]{1,0:T(8,128)(2,1)} %query_ref.1), channel_id=1, source_target_pairs={{0,8},{4,12},{8,0},{12,4},{16,24},{20,28},{24,16},{28,20},{1,9},{5... | collective-permute-start | bytes 1179656 | tf_op jit(solution)/shard_map/ppermute | solution.py:259
  1.2 2.6 %collective-permute-start.7 = (bf16[32,1024]{1,0:T(8,128)(2,1)}, bf16[32,1024]{1,0:T(8,128)(2,1)S(1)}, u32[]{:S(2)}, u32[]{:S(2)}) collective-permute-start(bf16[32,1024]{1,0:T(8,128)(2,1)} %value_refs_0_.3), channel_id=1, source_target_pairs={{0,4},{4,0},{8,12},{12,8},{16,20},{20,16},{24,28},{28,24},{1,5},{5... | collective-permute-start | bytes 196616 | tf_op jit(solution)/shard_map/ppermute | solution.py:259
  3.8 0.0 collective-permute-done.15
  3.8 0.9 %slice_select_fusion = bf16[16,6144]{1,0:T(8,128)(2,1)S(1)} fusion(bf16[32,6144]{1,0:T(8,128)(2,1)S(1)} %collective-permute-done.15, bf16[32,6144]{1,0:T(8,128)(2,1)} %query_ref.1, pred[]{:T(512)S(6)} %eq.13), kind=kLoop, calls=%fused_computation | loop fusion | flops 98304 | bytes 589825 | tf_op jit(solution)/shard_map/jit(_where)/select_n | solution.py:275
  4.7 0.0 copy-start.4
  4.7 0.0 copy-start.5
  4.7 0.0 copy-start.6
  4.8 0.0 copy-start.2
  4.8 0.0 copy-start.3
  4.8 1.9 %collective-permute-start.16 = (bf16[16,3072]{1,0:T(8,128)(2,1)S(1)}, bf16[16,3072]{1,0:T(8,128)(2,1)S(1)}, u32[]{:S(2)}, u32[]{:S(2)}) collective-permute-start(bf16[16,3072]{1,0:T(8,128)(2,1)S(1)} %broadcast_select_fusion.1), channel_id=1, source_target_pairs={{0,4},{4,0},{8,12},{12,8},{16,20},{20,16},{24,28},{28,24},{1,5},{5... | collective-permute-start | bytes 294920 | tf_op jit(solution)/shard_map/ppermute | solution.py:259
  6.7 0.0 copy-done.1
  6.7 0.0 copy-done.4
  6.7 0.0 copy-done.5
  6.7 0.0 copy-done.6
  6.7 0.6 %prepare.1 = (f32[2,3072]{1,0:T(2,128)S(1)}, f32[2,256]{1,0:T(2,128)S(1)}, f32[2,32,128]{2,1,0:T(8,128)S(1)}) custom-call(s32[4]{0:T(128)S(1)} %copy-done.5, s32[4,4]{1,0:T(4,128)S(1)} %copy-done.4, s32[4]{0:T(128)S(1)} %copy-done.6, f32[64,3072]{1,0:T(8,128)S(1)} %copy-done.1), custom_call_target="tpu_custom_call" | custom-call | tf_op jit(solution)/shard_map/prepare/pallas_call | solution.py:282
  7.3 0.0 copy-start
  7.4 0.6 %collective-permute-start.14 = (f32[2,3072]{1,0:T(2,128)S(1)}, f32[2,3072]{1,0:T(2,128)S(1)}, u32[]{:S(2)}, u32[]{:S(2)}) collective-permute-start(f32[2,3072]{1,0:T(2,128)S(1)} %get-tuple-element.7.gain_ref), channel_id=1, source_target_pairs={{0,4},{4,0},{8,12},{12,8},{16,20},{20,16},{24,28},{28,24},{1,5},{5... | collective-permute-start | bytes 73736 | tf_op jit(solution)/shard_map/ppermute | solution.py:259
  7.9 0.0 copy-done.2
  7.9 1.5 %collective-permute-start = (bf16[32,1024]{1,0:T(8,128)(2,1)S(1)}, bf16[32,1024]{1,0:T(8,128)(2,1)S(1)}, u32[]{:S(2)}, u32[]{:S(2)}) collective-permute-start(bf16[32,1024]{1,0:T(8,128)(2,1)S(1)} %copy-done.2), channel_id=1, source_target_pairs={{0,4},{4,0},{8,12},{12,8},{16,20},{20,16},{24,28},{28,24},{1,5},{5... | collective-permute-start | bytes 196616 | tf_op jit(solution)/shard_map/ppermute | solution.py:259
  9.4 0.0 copy-done.3
  9.4 1.5 %collective-permute-start.8 = (bf16[32,1024]{1,0:T(8,128)(2,1)S(1)}, bf16[32,1024]{1,0:T(8,128)(2,1)S(1)}, u32[]{:S(2)}, u32[]{:S(2)}) collective-permute-start(bf16[32,1024]{1,0:T(8,128)(2,1)S(1)} %copy-done.3), channel_id=1, source_target_pairs={{0,16},{4,20},{8,24},{12,28},{16,0},{20,4},{24,8},{28,12},{1,17},{... | collective-permute-start | bytes 196616 | tf_op jit(solution)/shard_map/ppermute | solution.py:259
  11.0 0.4 %collective-permute-done.14.far_gain_ref = f32[2,3072]{1,0:T(2,128)S(1)} collective-permute-done((f32[2,3072]{1,0:T(2,128)S(1)}, f32[2,3072]{1,0:T(2,128)S(1)}, u32[]{:S(2)}, u32[]{:S(2)}) %collective-permute-start.14) | collective-permute-done | bytes 24608 | tf_op jit(solution)/shard_map/ppermute | solution.py:259
  11.4 1.5 %collective-permute-start.1 = (bf16[32,1024]{1,0:T(8,128)(2,1)S(1)}, bf16[32,1024]{1,0:T(8,128)(2,1)S(1)}, u32[]{:S(2)}, u32[]{:S(2)}) collective-permute-start(bf16[32,1024]{1,0:T(8,128)(2,1)S(1)} %copy-done.2), channel_id=1, source_target_pairs={{0,16},{4,20},{8,24},{12,28},{16,0},{20,4},{24,8},{28,12},{1,17},{... | collective-permute-start | bytes 196616 | tf_op jit(solution)/shard_map/ppermute | solution.py:259
  12.9 0.0 collective-permute-done.7.value_refs_1_
  12.9 0.0 collective-permute-start.10
  12.9 0.0 collective-permute-done.key_refs_1_
  12.9 0.5 %collective-permute-start.3 = (bf16[32,1024]{1,0:T(8,128)(2,1)S(1)}, bf16[32,1024]{1,0:T(8,128)(2,1)S(1)}, u32[]{:S(2)}, u32[]{:S(2)}) collective-permute-start(bf16[32,1024]{1,0:T(8,128)(2,1)S(1)} %copy-done.2), channel_id=1, source_target_pairs={{0,8},{4,12},{8,0},{12,4},{16,24},{20,28},{24,16},{28,20},{1,9},{5... | collective-permute-start | bytes 196616 | tf_op jit(solution)/shard_map/ppermute | solution.py:259
  13.4 0.7 %collective-permute-done.8.value_refs_2_ = bf16[32,1024]{1,0:T(8,128)(2,1)S(1)} collective-permute-done((bf16[32,1024]{1,0:T(8,128)(2,1)S(1)}, bf16[32,1024]{1,0:T(8,128)(2,1)S(1)}, u32[]{:S(2)}, u32[]{:S(2)}) %collective-permute-start.8) | collective-permute-done | bytes 65568 | tf_op jit(solution)/shard_map/ppermute | solution.py:259
  14.1 1.7 %collective-permute-start.9 = (bf16[32,1024]{1,0:T(8,128)(2,1)S(1)}, bf16[32,1024]{1,0:T(8,128)(2,1)S(1)}, u32[]{:S(2)}, u32[]{:S(2)}) collective-permute-start(bf16[32,1024]{1,0:T(8,128)(2,1)S(1)} %collective-permute-done.7.value_refs_1_), channel_id=1, source_target_pairs={{0,16},{4,20},{8,24},{12,28},{16,0},{20,4},{24,8},{28,12},{1,17},{... | collective-permute-start | bytes 196616 | tf_op jit(solution)/shard_map/ppermute | solution.py:259
  15.9 0.0 collective-permute-done.1.key_refs_2_
  15.9 0.0 collective-permute-start.11
  15.9 0.0 collective-permute-done.10.value_refs_4_
  15.9 1.6 %collective-permute-start.2 = (bf16[32,1024]{1,0:T(8,128)(2,1)S(1)}, bf16[32,1024]{1,0:T(8,128)(2,1)S(1)}, u32[]{:S(2)}, u32[]{:S(2)}) collective-permute-start(bf16[32,1024]{1,0:T(8,128)(2,1)S(1)} %collective-permute-done.key_refs_1_), channel_id=1, source_target_pairs={{0,16},{4,20},{8,24},{12,28},{16,0},{20,4},{24,8},{28,12},{1,17},{... | collective-permute-start | bytes 196616 | tf_op jit(solution)/shard_map/ppermute | solution.py:259
  17.5 0.0 collective-permute-done.16.query_refs_1_
  17.5 0.2 collective-permute-start.4
  17.7 0.0 collective-permute-done.3.key_refs_4_
  17.7 0.5 %collective-permute-start.17 = (bf16[16,3072]{1,0:T(8,128)(2,1)S(1)}, bf16[16,3072]{1,0:T(8,128)(2,1)S(1)}, u32[]{:S(2)}, u32[]{:S(2)}) collective-permute-start(bf16[16,3072]{1,0:T(8,128)(2,1)S(1)} %get-tuple-element.8), channel_id=1, source_target_pairs={{0,16},{4,20},{8,24},{12,28},{16,0},{20,4},{24,8},{28,12},{1,17},{... | collective-permute-start | bytes 294920 | tf_op jit(solution)/shard_map/ppermute | solution.py:259
  18.2 0.2 collective-permute-done.9.value_refs_3_
  18.4 0.0 collective-permute-start.12
  18.4 2.0 %collective-permute-done.2.key_refs_3_ = bf16[32,1024]{1,0:T(8,128)(2,1)S(1)} collective-permute-done((bf16[32,1024]{1,0:T(8,128)(2,1)S(1)}, bf16[32,1024]{1,0:T(8,128)(2,1)S(1)}, u32[]{:S(2)}, u32[]{:S(2)}) %collective-permute-start.2) | collective-permute-done | bytes 65568 | tf_op jit(solution)/shard_map/ppermute | solution.py:259
  20.4 0.0 collective-permute-start.5
  20.4 0.0 collective-permute-done.11.value_refs_5_
  20.4 0.5 %collective-permute-start.13 = (bf16[32,1024]{1,0:T(8,128)(2,1)S(1)}, bf16[32,1024]{1,0:T(8,128)(2,1)S(1)}, u32[]{:S(2)}, u32[]{:S(2)}) collective-permute-start(bf16[32,1024]{1,0:T(8,128)(2,1)S(1)} %collective-permute-done.9.value_refs_3_), channel_id=1, source_target_pairs={{0,8},{4,12},{8,0},{12,4},{16,24},{20,28},{24,16},{28,20},{1,9},{5... | collective-permute-start | bytes 196616 | tf_op jit(solution)/shard_map/ppermute | solution.py:259
  20.9 0.0 collective-permute-done.4.key_refs_5_
  20.9 0.1 collective-permute-start.6
  21.0 0.0 collective-permute-done.12.value_refs_6_
  21.0 0.7 %collective-permute-done.5.key_refs_6_ = bf16[32,1024]{1,0:T(8,128)(2,1)S(1)} collective-permute-done((bf16[32,1024]{1,0:T(8,128)(2,1)S(1)}, bf16[32,1024]{1,0:T(8,128)(2,1)S(1)}, u32[]{:S(2)}, u32[]{:S(2)}) %collective-permute-start.5) | collective-permute-done | bytes 65568 | tf_op jit(solution)/shard_map/ppermute | solution.py:259
  21.6 0.2 collective-permute-done.13.value_refs_7_
  21.8 0.4 %collective-permute-done.6.key_refs_7_ = bf16[32,1024]{1,0:T(8,128)(2,1)S(1)} collective-permute-done((bf16[32,1024]{1,0:T(8,128)(2,1)S(1)}, bf16[32,1024]{1,0:T(8,128)(2,1)S(1)}, u32[]{:S(2)}, u32[]{:S(2)}) %collective-permute-start.6) | collective-permute-done | bytes 65568 | tf_op jit(solution)/shard_map/ppermute | solution.py:259
  22.2 0.0 copy-done
  22.2 1.8 %attention.1 = bf16[32,6144]{1,0:T(8,128)(2,1)} custom-call(bf16[32,6144]{1,0:T(8,128)(2,1)S(1)} %copy-done, bf16[32,1024]{1,0:T(8,128)(2,1)S(1)} %copy-done.2, bf16[32,1024]{1,0:T(8,128)(2,1)S(1)} %collective-permute-done.key_refs_1_, bf16[32,1024]{1,0:T(8,128)(2,1)S(1)} %collective-permute-done.1.key_refs_2_, ...), custom_call_target="tpu_custom_call" | custom-call | tf_op jit(solution)/shard_map/attention/pallas_call | solution.py:296
  23.9 0.0 collective-permute-done.17.query_refs_2_
  23.9 1.5 %first_clip.1 = bf16[16,3072]{1,0:T(8,128)(2,1)} custom-call(bf16[16,3072]{1,0:T(8,128)(2,1)S(1)} %get-tuple-element.9.query_refs_0_, bf16[16,3072]{1,0:T(8,128)(2,1)S(1)} %collective-permute-done.16.query_refs_1_, bf16[16,3072]{1,0:T(8,128)(2,1)S(1)} %collective-permute-done.17.query_refs_2_, bf16[32,1024]{1,0:T(8,128)(2,1)S(1)} %copy-done.2, ...), custom_call_target="tpu_custom_call" | custom-call | tf_op jit(solution)/shard_map/first_clip/pallas_call | solution.py:304
  (2 shorter events, 0.0 us)
Async XLA Ops:
  0.6 6.1 %copy-start.1 = (f32[64,3072]{1,0:T(8,128)S(1)}, f32[64,3072]{1,0:T(8,128)}, u32[]{:S(2)}) copy-start(f32[64,3072]{1,0:T(8,128)} %gain_ref.1) | copy-start | bytes 2359300
  0.6 3.1 %collective-permute-start.15 = (bf16[32,6144]{1,0:T(8,128)(2,1)}, bf16[32,6144]{1,0:T(8,128)(2,1)S(1)}, u32[]{:S(2)}, u32[]{:S(2)}) collective-permute-start(bf16[32,6144]{1,0:T(8,128)(2,1)} %query_ref.1), channel_id=1, source_target_pairs={{0,8},{4,12},{8,0},{12,4},{16,24},{20,28},{24,16},{28,20},{1,9},{5... | collective-permute-start | bytes 1179656 | tf_op jit(solution)/shard_map/ppermute | solution.py:259
  1.2 11.7 %collective-permute-start.7 = (bf16[32,1024]{1,0:T(8,128)(2,1)}, bf16[32,1024]{1,0:T(8,128)(2,1)S(1)}, u32[]{:S(2)}, u32[]{:S(2)}) collective-permute-start(bf16[32,1024]{1,0:T(8,128)(2,1)} %value_refs_0_.3), channel_id=1, source_target_pairs={{0,4},{4,0},{8,12},{12,8},{16,20},{20,16},{24,28},{28,24},{1,5},{5... | collective-permute-start | bytes 196616 | tf_op jit(solution)/shard_map/ppermute | solution.py:259
  4.7 2.0 %copy-start.4 = (s32[4,4]{1,0:T(4,128)S(1)}, s32[4,4]{1,0:T(4,128)}, u32[]{:S(2)}) copy-start(s32[4,4]{1,0:T(4,128)} %visible_ref.1) | copy-start | bytes 196
  4.7 2.0 %copy-start.5 = (s32[4]{0:T(128)S(1)}, s32[4]{0:T(128)}, u32[]{:S(2)}) copy-start(s32[4]{0:T(128)} %levels_ref.1) | copy-start | bytes 52
  4.7 2.0 %copy-start.6 = (s32[4]{0:T(128)S(1)}, s32[4]{0:T(128)}, u32[]{:S(2)}) copy-start(s32[4]{0:T(128)} %counts_ref.1) | copy-start | bytes 52
  4.8 3.2 %copy-start.2 = (bf16[32,1024]{1,0:T(8,128)(2,1)S(1)}, bf16[32,1024]{1,0:T(8,128)(2,1)}, u32[]{:S(2)}) copy-start(bf16[32,1024]{1,0:T(8,128)(2,1)} %key_refs_0_.3) | copy-start | bytes 196612
  4.8 4.7 %copy-start.3 = (bf16[32,1024]{1,0:T(8,128)(2,1)S(1)}, bf16[32,1024]{1,0:T(8,128)(2,1)}, u32[]{:S(2)}) copy-start(bf16[32,1024]{1,0:T(8,128)(2,1)} %value_refs_0_.3) | copy-start | bytes 196612
  4.8 12.7 %collective-permute-start.16 = (bf16[16,3072]{1,0:T(8,128)(2,1)S(1)}, bf16[16,3072]{1,0:T(8,128)(2,1)S(1)}, u32[]{:S(2)}, u32[]{:S(2)}) collective-permute-start(bf16[16,3072]{1,0:T(8,128)(2,1)S(1)} %broadcast_select_fusion.1), channel_id=1, source_target_pairs={{0,4},{4,0},{8,12},{12,8},{16,20},{20,16},{24,28},{28,24},{1,5},{5... | collective-permute-start | bytes 294920 | tf_op jit(solution)/shard_map/ppermute | solution.py:259
  7.3 14.8 %copy-start = (bf16[32,6144]{1,0:T(8,128)(2,1)S(1)}, bf16[32,6144]{1,0:T(8,128)(2,1)}, u32[]{:S(2)}) copy-start(bf16[32,6144]{1,0:T(8,128)(2,1)} %query_ref.1) | copy-start | bytes 1179652
  7.4 4.0 %collective-permute-start.14 = (f32[2,3072]{1,0:T(2,128)S(1)}, f32[2,3072]{1,0:T(2,128)S(1)}, u32[]{:S(2)}, u32[]{:S(2)}) collective-permute-start(f32[2,3072]{1,0:T(2,128)S(1)} %get-tuple-element.7.gain_ref), channel_id=1, source_target_pairs={{0,4},{4,0},{8,12},{12,8},{16,20},{20,16},{24,28},{28,24},{1,5},{5... | collective-permute-start | bytes 73736 | tf_op jit(solution)/shard_map/ppermute | solution.py:259
  7.9 4.9 %collective-permute-start = (bf16[32,1024]{1,0:T(8,128)(2,1)S(1)}, bf16[32,1024]{1,0:T(8,128)(2,1)S(1)}, u32[]{:S(2)}, u32[]{:S(2)}) collective-permute-start(bf16[32,1024]{1,0:T(8,128)(2,1)S(1)} %copy-done.2), channel_id=1, source_target_pairs={{0,4},{4,0},{8,12},{12,8},{16,20},{20,16},{24,28},{28,24},{1,5},{5... | collective-permute-start | bytes 196616 | tf_op jit(solution)/shard_map/ppermute | solution.py:259
  9.4 4.7 %collective-permute-start.8 = (bf16[32,1024]{1,0:T(8,128)(2,1)S(1)}, bf16[32,1024]{1,0:T(8,128)(2,1)S(1)}, u32[]{:S(2)}, u32[]{:S(2)}) collective-permute-start(bf16[32,1024]{1,0:T(8,128)(2,1)S(1)} %copy-done.3), channel_id=1, source_target_pairs={{0,16},{4,20},{8,24},{12,28},{16,0},{20,4},{24,8},{28,12},{1,17},{... | collective-permute-start | bytes 196616 | tf_op jit(solution)/shard_map/ppermute | solution.py:259
  11.4 4.5 %collective-permute-start.1 = (bf16[32,1024]{1,0:T(8,128)(2,1)S(1)}, bf16[32,1024]{1,0:T(8,128)(2,1)S(1)}, u32[]{:S(2)}, u32[]{:S(2)}) collective-permute-start(bf16[32,1024]{1,0:T(8,128)(2,1)S(1)} %copy-done.2), channel_id=1, source_target_pairs={{0,16},{4,20},{8,24},{12,28},{16,0},{20,4},{24,8},{28,12},{1,17},{... | collective-permute-start | bytes 196616 | tf_op jit(solution)/shard_map/ppermute | solution.py:259
  12.9 3.0 %collective-permute-start.10 = (bf16[32,1024]{1,0:T(8,128)(2,1)S(1)}, bf16[32,1024]{1,0:T(8,128)(2,1)S(1)}, u32[]{:S(2)}, u32[]{:S(2)}) collective-permute-start(bf16[32,1024]{1,0:T(8,128)(2,1)S(1)} %copy-done.3), channel_id=1, source_target_pairs={{0,8},{4,12},{8,0},{12,4},{16,24},{20,28},{24,16},{28,20},{1,9},{5... | collective-permute-start | bytes 196616 | tf_op jit(solution)/shard_map/ppermute | solution.py:259
  12.9 4.8 %collective-permute-start.3 = (bf16[32,1024]{1,0:T(8,128)(2,1)S(1)}, bf16[32,1024]{1,0:T(8,128)(2,1)S(1)}, u32[]{:S(2)}, u32[]{:S(2)}) collective-permute-start(bf16[32,1024]{1,0:T(8,128)(2,1)S(1)} %copy-done.2), channel_id=1, source_target_pairs={{0,8},{4,12},{8,0},{12,4},{16,24},{20,28},{24,16},{28,20},{1,9},{5... | collective-permute-start | bytes 196616 | tf_op jit(solution)/shard_map/ppermute | solution.py:259
  14.1 4.3 %collective-permute-start.9 = (bf16[32,1024]{1,0:T(8,128)(2,1)S(1)}, bf16[32,1024]{1,0:T(8,128)(2,1)S(1)}, u32[]{:S(2)}, u32[]{:S(2)}) collective-permute-start(bf16[32,1024]{1,0:T(8,128)(2,1)S(1)} %collective-permute-done.7.value_refs_1_), channel_id=1, source_target_pairs={{0,16},{4,20},{8,24},{12,28},{16,0},{20,4},{24,8},{28,12},{1,17},{... | collective-permute-start | bytes 196616 | tf_op jit(solution)/shard_map/ppermute | solution.py:259
  15.9 4.5 %collective-permute-start.11 = (bf16[32,1024]{1,0:T(8,128)(2,1)S(1)}, bf16[32,1024]{1,0:T(8,128)(2,1)S(1)}, u32[]{:S(2)}, u32[]{:S(2)}) collective-permute-start(bf16[32,1024]{1,0:T(8,128)(2,1)S(1)} %collective-permute-done.7.value_refs_1_), channel_id=1, source_target_pairs={{0,8},{4,12},{8,0},{12,4},{16,24},{20,28},{24,16},{28,20},{1,9},{5... | collective-permute-start | bytes 196616 | tf_op jit(solution)/shard_map/ppermute | solution.py:259
  15.9 4.5 %collective-permute-start.2 = (bf16[32,1024]{1,0:T(8,128)(2,1)S(1)}, bf16[32,1024]{1,0:T(8,128)(2,1)S(1)}, u32[]{:S(2)}, u32[]{:S(2)}) collective-permute-start(bf16[32,1024]{1,0:T(8,128)(2,1)S(1)} %collective-permute-done.key_refs_1_), channel_id=1, source_target_pairs={{0,16},{4,20},{8,24},{12,28},{16,0},{20,4},{24,8},{28,12},{1,17},{... | collective-permute-start | bytes 196616 | tf_op jit(solution)/shard_map/ppermute | solution.py:259
  17.5 3.4 %collective-permute-start.4 = (bf16[32,1024]{1,0:T(8,128)(2,1)S(1)}, bf16[32,1024]{1,0:T(8,128)(2,1)S(1)}, u32[]{:S(2)}, u32[]{:S(2)}) collective-permute-start(bf16[32,1024]{1,0:T(8,128)(2,1)S(1)} %collective-permute-done.key_refs_1_), channel_id=1, source_target_pairs={{0,8},{4,12},{8,0},{12,4},{16,24},{20,28},{24,16},{28,20},{1,9},{5... | collective-permute-start | bytes 196616 | tf_op jit(solution)/shard_map/ppermute | solution.py:259
  17.7 6.2 %collective-permute-start.17 = (bf16[16,3072]{1,0:T(8,128)(2,1)S(1)}, bf16[16,3072]{1,0:T(8,128)(2,1)S(1)}, u32[]{:S(2)}, u32[]{:S(2)}) collective-permute-start(bf16[16,3072]{1,0:T(8,128)(2,1)S(1)} %get-tuple-element.8), channel_id=1, source_target_pairs={{0,16},{4,20},{8,24},{12,28},{16,0},{20,4},{24,8},{28,12},{1,17},{... | collective-permute-start | bytes 294920 | tf_op jit(solution)/shard_map/ppermute | solution.py:259
  18.4 2.6 %collective-permute-start.12 = (bf16[32,1024]{1,0:T(8,128)(2,1)S(1)}, bf16[32,1024]{1,0:T(8,128)(2,1)S(1)}, u32[]{:S(2)}, u32[]{:S(2)}) collective-permute-start(bf16[32,1024]{1,0:T(8,128)(2,1)S(1)} %collective-permute-done.8.value_refs_2_), channel_id=1, source_target_pairs={{0,8},{4,12},{8,0},{12,4},{16,24},{20,28},{24,16},{28,20},{1,9},{5... | collective-permute-start | bytes 196616 | tf_op jit(solution)/shard_map/ppermute | solution.py:259
  20.4 1.3 %collective-permute-start.5 = (bf16[32,1024]{1,0:T(8,128)(2,1)S(1)}, bf16[32,1024]{1,0:T(8,128)(2,1)S(1)}, u32[]{:S(2)}, u32[]{:S(2)}) collective-permute-start(bf16[32,1024]{1,0:T(8,128)(2,1)S(1)} %collective-permute-done.1.key_refs_2_), channel_id=1, source_target_pairs={{0,8},{4,12},{8,0},{12,4},{16,24},{20,28},{24,16},{28,20},{1,9},{5... | collective-permute-start | bytes 196616 | tf_op jit(solution)/shard_map/ppermute | solution.py:259
  20.4 1.4 %collective-permute-start.13 = (bf16[32,1024]{1,0:T(8,128)(2,1)S(1)}, bf16[32,1024]{1,0:T(8,128)(2,1)S(1)}, u32[]{:S(2)}, u32[]{:S(2)}) collective-permute-start(bf16[32,1024]{1,0:T(8,128)(2,1)S(1)} %collective-permute-done.9.value_refs_3_), channel_id=1, source_target_pairs={{0,8},{4,12},{8,0},{12,4},{16,24},{20,28},{24,16},{28,20},{1,9},{5... | collective-permute-start | bytes 196616 | tf_op jit(solution)/shard_map/ppermute | solution.py:259
  20.9 1.3 %collective-permute-start.6 = (bf16[32,1024]{1,0:T(8,128)(2,1)S(1)}, bf16[32,1024]{1,0:T(8,128)(2,1)S(1)}, u32[]{:S(2)}, u32[]{:S(2)}) collective-permute-start(bf16[32,1024]{1,0:T(8,128)(2,1)S(1)} %collective-permute-done.2.key_refs_3_), channel_id=1, source_target_pairs={{0,8},{4,12},{8,0},{12,4},{16,24},{20,28},{24,16},{28,20},{1,9},{5... | collective-permute-start | bytes 196616 | tf_op jit(solution)/shard_map/ppermute | solution.py:259
